TPU v7x, 32 devices: a whole 2x2x4 slice. The times are simulated.
32 devices in a mesh: blk: 4 (over z), slab: 8 (over y, x, core).
Axes of the slice: x: 2, y: 2, z: 4, core: 2. Of those that a mesh axis runs over, the one named last changes fastest.
Arguments:
- new_rows: bfloat16 [16384, 768], P(('blk', 'slab')), may hold values from -6 to 6
- index_rows: bfloat16 [16384, 768], P('blk'), may hold values from -6 to 6
- pattern: int32 [32, 4], replicated, may hold values from 0 to 1, as said below
- kept_row: int32 [8192], P(('blk', 'slab')), may hold values from 0 to 511
- kept_owner: int32 [8192, 1], P(('blk', 'slab')), may hold values from 0 to 31; in each aligned block of 256 rows (0 to 255, 256 to 511, ...) at most 16 rows name the same one
- kept_local: int32 [8192], P(('blk', 'slab')), may hold values from 0 to 15
Outputs:
- best_cosine: float32 [16384], P(('blk', 'slab'))
- centroid_sums: float32 [512, 768], P(('blk', 'slab'))
- kept_counts: float32 [512], P(('blk', 'slab'))
Inputs may be any that keep to these rules, and one draw needn't show every extreme that they name: `pattern`: every row has at least one 1. `kept_owner`: the 256 entries of one device name one owner at most 16 times, a bound that some block reaches.
All inputs are finite; a program needn't handle non-finite values.
Results may differ from a plain program's by a relative error of at most 0.0029.
Values may be sent and summed in bfloat16 or wider, within the bound.
No kernel may reach another device: no remote copies, remote signals or barrier semaphores. Data moves between devices by JAX's collectives and lax.ppermute only.
A program may use at most 64 MiB of HBM per device.

v0:
```python
import jax
import jax.numpy as jnp
from jax import lax
from jax.sharding import PartitionSpec as P

CL_DEV = 16


EPS = 1e-06


def shifted(value, axis, steps):
    count = lax.axis_size(axis)
    pairs = [(source, (source + steps) % count) for source in range(count)]
    return lax.ppermute(value, axis, pairs)


def unit_rows(values):
    wide = values.astype(jnp.float32)
    scale = lax.rsqrt(jnp.sum(wide * wide, axis=-1, keepdims=True) + EPS)
    return (wide * scale).astype(jnp.bfloat16)


def per_device(new_rows, index_rows, pattern, kept_row, kept_owner, kept_local):
    cycle = lax.axis_size("blk")
    lanes = lax.axis_size("slab")
    here = lax.axis_index("blk")
    lane = lax.axis_index("slab")
    new_unit = unit_rows(new_rows)
    index_unit = unit_rows(index_rows)

    def tile_max(rows, offset):
        anchor = (here - offset) % cycle
        active = pattern[anchor * lanes + lane, here] > 0
        scores = lax.dot_general(
            rows, index_unit, (((1,), (1,)), ((), ())), preferred_element_type=jnp.float32
        )
        return jnp.where(active, jnp.max(scores, axis=1), jnp.float32(-2.0))

    slots = {0: tile_max(new_unit, 0)}
    ahead_steps = cycle - 1
    moving = new_unit
    for step in range(1, ahead_steps + 1):
        moving = shifted(moving, "blk", 1)
        slots[step] = tile_max(moving, step)
    stacked = jnp.stack([slots[offset] for offset in range(cycle)], axis=0)
    order = (here - jnp.arange(cycle, dtype=jnp.int32)) % cycle
    by_anchor = jnp.take(stacked, order, axis=0)
    returned = lax.all_to_all(by_anchor, "blk", split_axis=0, concat_axis=0, tiled=True)
    best = jnp.max(returned, axis=0)
    picked = new_unit[kept_row]
    owner = kept_owner[:, 0]
    devices = cycle * lanes
    entries = kept_row.shape[0]
    local_tags = (kept_local[:, None] == jnp.arange(CL_DEV, dtype=jnp.int32)[None, :]).astype(
        jnp.bfloat16
    )
    capacity = (entries + devices - 1) // devices * 2
    position = jnp.arange(entries, dtype=jnp.int32)
    same_owner = owner[:, None] == owner[None, :]
    earlier = position[:, None] > position[None, :]
    rank = jnp.sum((same_owner & earlier).astype(jnp.int32), axis=1)
    target = owner * capacity + rank
    placing = (jnp.arange(devices * capacity, dtype=jnp.int32)[:, None] == target[None, :]).astype(
        jnp.bfloat16
    )
    payload = jnp.dot(placing, picked, preferred_element_type=jnp.float32).astype(jnp.bfloat16)
    tagging = jnp.dot(placing, local_tags, preferred_element_type=jnp.float32).astype(jnp.bfloat16)
    got_rows, got_tags = (
        lax.all_to_all(payload, ("blk", "slab"), split_axis=0, concat_axis=0, tiled=True),
        lax.all_to_all(tagging, ("blk", "slab"), split_axis=0, concat_axis=0, tiled=True),
    )
    sums = lax.dot_general(
        got_tags, got_rows, (((0,), (0,)), ((), ())), preferred_element_type=jnp.float32
    )
    counts = jnp.sum(got_tags.astype(jnp.float32), axis=0)
    return (best, sums, counts)


def solution(mesh):
    placed = (
        P(("blk", "slab"), None),
        P("blk", None),
        P(),
        P(("blk", "slab")),
        P(("blk", "slab"), None),
        P(("blk", "slab")),
    )
    return jax.shard_map(
        per_device,
        mesh=mesh,
        in_specs=placed,
        out_specs=(P(("blk", "slab")), P(("blk", "slab"), None), P(("blk", "slab"))),
        check_vma=False,
    )
```

profile of v0, /device:TPU:0, one launch (start us, length us, event | category | flops | bytes accessed | tf_op | source)
XLA Modules:
  0.0 105.2 jit_solution(12683423208856667644)
XLA Ops:
  0.6 0.9 convert_reduce_fusion.1
  1.6 0.7 multiply_add_fusion
  2.3 0.9 convolution_convert_fusion.1
  3.3 0.7 reshape.177
  4.1 7.3 %all-to-all-start.1 = ((bf16[32,2,128]{2,1,0:T(2,128)(2,1)}), bf16[32,2,128]{2,1,0:T(2,128)(2,1)S(1)}, u32[]{:S(2)}, u32[]{:S(2)}) async-start(bf16[32,2,128]{2,1,0:T(2,128)(2,1)} %reshape.177), calls=%async_computation.1 | async-start | bytes 32768 | tf_op jit(solution)/shard_map/all_to_all | solution.py:71
  11.4 1.4 %fusion.2 = f32[512]{0:T(512)S(1)} fusion(bf16[512,768]{1,0:T(8,128)(2,1)} %param.6), kind=kLoop, calls=%fused_computation.12 | loop fusion | flops 1179136 | bytes 788480 | tf_op jit(solution)/shard_map/reduce_sum | solution.py:20
  12.8 1.3 %fusion.3 = bf16[512,768]{1,0:T(8,128)(2,1)S(1)} fusion(bf16[512,768]{1,0:T(8,128)(2,1)} %param.6, f32[512]{0:T(512)S(1)} %add_rsqrt_fusion.1), kind=kLoop, calls=%fused_computation.13 | loop fusion | flops 1179648 | bytes 1574912 | tf_op jit(solution)/shard_map/convert_element_type | solution.py:21
  14.1 1.8 %collective-permute-start = (bf16[512,768]{1,0:T(8,128)(2,1)S(1)}, bf16[512,768]{1,0:T(8,128)(2,1)S(1)}, u32[]{:S(2)}, u32[]{:S(2)}) collective-permute-start(bf16[512,768]{1,0:T(8,128)(2,1)S(1)} %fusion.3), channel_id=1, source_target_pairs={{0,8},{8,16},{16,24},{24,0},{1,9},{9,17},{17,25},{25,1},{2,10},{10... | collective-permute-start | bytes 2359304 | tf_op jit(solution)/shard_map/ppermute | solution.py:15
  15.9 0.8 compare_select_fusion
  16.8 4.2 %fusion = f32[4096]{0:T(1024)S(1)} fusion(bf16[4096,768]{1,0:T(8,128)(2,1)} %param.7), kind=kLoop, calls=%fused_computation.4 | loop fusion | flops 9433088 | bytes 6307840 | tf_op jit(solution)/shard_map/reduce_sum | solution.py:20
  21.1 4.0 %convolution_reduce_fusion.3 = f32[512]{0:T(512)S(1)} fusion(bf16[512,768]{1,0:T(8,128)(2,1)S(1)} %fusion.3, bf16[4096,768]{1,0:T(8,128)(2,1)S(1)} %copy-done, f32[4096]{0:T(1024)S(1)} %add_rsqrt_fusion), kind=kOutput, calls=%fused_computation.9 | convolution fusion | flops 3232759296 | bytes 7096320 | tf_op jit(solution)/shard_map/dot_general | solution.py:35
  25.1 1.2 %gather_fusion.1 = bf16[256,768]{1,0:T(8,128)(2,1)S(1)} fusion(bf16[512,768]{1,0:T(8,128)(2,1)S(1)} %fusion.3, s32[1024]{0:T(1024)S(1)} %pad_clamp_fusion), kind=kCustom, calls=%fused_computation.1 | custom fusion | bytes 787456 | tf_op jit(solution)/shard_map/gather | solution.py:51
  27.6 1.3 %convolution_convert_fusion = bf16[512,768]{1,0:T(8,128)(2,1)} fusion(bf16[256,768]{1,0:T(8,128)(2,1)S(1)} %gather_fusion.1, s32[256]{0:T(256)S(1)} %multiply_add_fusion), kind=kOutput, calls=%fused_computation.14 | convolution fusion | flops 201850880 | bytes 1180672 | tf_op jit(solution)/shard_map/dot_general | solution.py:67
  30.8 4.6 %all-to-all-start.2 = ((bf16[32,16,768]{2,1,0:T(8,128)(2,1)}), bf16[32,16,768]{2,1,0:T(8,128)(2,1)S(1)}, u32[]{:S(2)}, u32[]{:S(2)}) async-start(bf16[32,16,768]{2,1,0:T(8,128)(2,1)} %bitcast.12), calls=%async_computation.2 | async-start | bytes 1572864 | tf_op jit(solution)/shard_map/all_to_all | solution.py:70
  36.1 1.8 %collective-permute-start.1 = (bf16[512,768]{1,0:T(8,128)(2,1)S(1)}, bf16[512,768]{1,0:T(8,128)(2,1)S(1)}, u32[]{:S(2)}, u32[]{:S(2)}) collective-permute-start(bf16[512,768]{1,0:T(8,128)(2,1)S(1)} %collective-permute-done), channel_id=1, source_target_pairs={{0,8},{8,16},{16,24},{24,0},{1,9},{9,17},{17,25},{25,1},{2,10},{10... | collective-permute-start | bytes 2359304 | tf_op jit(solution)/shard_map/ppermute | solution.py:15
  37.9 6.5 %convolution_reduce_fusion.2 = f32[512]{0:T(512)S(1)} fusion(bf16[512,768]{1,0:T(8,128)(2,1)S(1)} %collective-permute-done, bf16[4096,768]{1,0:T(8,128)(2,1)} %param.7, f32[4096]{0:T(1024)S(1)} %add_rsqrt_fusion), kind=kOutput, calls=%fused_computation.8 | convolution fusion | flops 3232759296 | bytes 7096320 | tf_op jit(solution)/shard_map/dot_general | solution.py:35
  44.4 25.2 %collective-permute-done.1 = bf16[512,768]{1,0:T(8,128)(2,1)S(1)} collective-permute-done((bf16[512,768]{1,0:T(8,128)(2,1)S(1)}, bf16[512,768]{1,0:T(8,128)(2,1)S(1)}, u32[]{:S(2)}, u32[]{:S(2)}) %collective-permute-start.1) | collective-permute-done | bytes 786464 | tf_op jit(solution)/shard_map/ppermute | solution.py:15
  69.6 1.7 %collective-permute-start.2 = (bf16[512,768]{1,0:T(8,128)(2,1)S(1)}, bf16[512,768]{1,0:T(8,128)(2,1)S(1)}, u32[]{:S(2)}, u32[]{:S(2)}) collective-permute-start(bf16[512,768]{1,0:T(8,128)(2,1)S(1)} %collective-permute-done.1), channel_id=1, source_target_pairs={{0,8},{8,16},{16,24},{24,0},{1,9},{9,17},{17,25},{25,1},{2,10},{10... | collective-permute-start | bytes 2359304 | tf_op jit(solution)/shard_map/ppermute | solution.py:15
  71.3 4.0 %convolution_reduce_fusion.1 = f32[512]{0:T(512)S(1)} fusion(bf16[512,768]{1,0:T(8,128)(2,1)S(1)} %collective-permute-done.1, bf16[4096,768]{1,0:T(8,128)(2,1)S(1)} %bitcast.25, f32[4096]{0:T(1024)S(1)} %add_rsqrt_fusion), kind=kOutput, calls=%fused_computation.7 | convolution fusion | flops 3232759296 | bytes 7096320 | tf_op jit(solution)/shard_map/dot_general | solution.py:35
  75.3 15.1 %collective-permute-done.2 = bf16[512,768]{1,0:T(8,128)(2,1)S(1)} collective-permute-done((bf16[512,768]{1,0:T(8,128)(2,1)S(1)}, bf16[512,768]{1,0:T(8,128)(2,1)S(1)}, u32[]{:S(2)}, u32[]{:S(2)}) %collective-permute-start.2) | collective-permute-done | bytes 786464 | tf_op jit(solution)/shard_map/ppermute | solution.py:15
  90.4 4.0 %convolution_reduce_fusion = f32[512]{0:T(512)S(1)} fusion(bf16[512,768]{1,0:T(8,128)(2,1)S(1)} %collective-permute-done.2, bf16[4096,768]{1,0:T(8,128)(2,1)S(1)} %bitcast.25, f32[4096]{0:T(1024)S(1)} %add_rsqrt_fusion), kind=kOutput, calls=%fused_computation.6 | convolution fusion | flops 3232759296 | bytes 7096320 | tf_op jit(solution)/shard_map/dot_general | solution.py:35
  95.6 3.4 %all-to-all-start = ((f32[4,1,512]{2,1,0:T(1,128)}), f32[4,1,512]{2,1,0:T(1,128)S(1)}, u32[]{:S(2)}, u32[]{:S(2)}) async-start(f32[4,1,512]{2,1,0:T(1,128)} %copy.17), calls=%async_computation | async-start | bytes 16384 | tf_op jit(solution)/shard_map/all_to_all | solution.py:49
  99.1 0.9 convolution_bitcast_fusion
  99.9 4.7 %all-to-all-done = f32[4,1,512]{2,1,0:T(1,128)S(1)} async-done(((f32[4,1,512]{2,1,0:T(1,128)}), f32[4,1,512]{2,1,0:T(1,128)S(1)}, u32[]{:S(2)}, u32[]{:S(2)}) %all-to-all-start) | async-done | bytes 8224 | tf_op jit(solution)/shard_map/all_to_all | solution.py:49
  (31 shorter events, 3.5 us)
Async XLA Ops:
  4.1 26.7 %all-to-all-start.1 = ((bf16[32,2,128]{2,1,0:T(2,128)(2,1)}), bf16[32,2,128]{2,1,0:T(2,128)(2,1)S(1)}, u32[]{:S(2)}, u32[]{:S(2)}) async-start(bf16[32,2,128]{2,1,0:T(2,128)(2,1)} %reshape.177), calls=%async_computation.1 | async-start | bytes 32768 | tf_op jit(solution)/shard_map/all_to_all | solution.py:71
  14.1 22.0 %collective-permute-start = (bf16[512,768]{1,0:T(8,128)(2,1)S(1)}, bf16[512,768]{1,0:T(8,128)(2,1)S(1)}, u32[]{:S(2)}, u32[]{:S(2)}) collective-permute-start(bf16[512,768]{1,0:T(8,128)(2,1)S(1)} %fusion.3), channel_id=1, source_target_pairs={{0,8},{8,16},{16,24},{24,0},{1,9},{9,17},{17,25},{25,1},{2,10},{10... | collective-permute-start | bytes 2359304 | tf_op jit(solution)/shard_map/ppermute | solution.py:15
  15.9 5.1 %copy-start = (bf16[4096,768]{1,0:T(8,128)(2,1)S(1)}, bf16[4096,768]{1,0:T(8,128)(2,1)}, u32[]{:S(2)}) copy-start(bf16[4096,768]{1,0:T(8,128)(2,1)} %param.7) | copy-start | bytes 18874372
  21.1 5.2 %copy-start.1 = (s32[32,4]{0,1:T(4,128)S(1)}, s32[32,4]{0,1:T(4,128)}, u32[]{:S(2)}) copy-start(s32[32,4]{0,1:T(4,128)} %param.8) | copy-start | bytes 1540
  30.8 64.9 %all-to-all-start.2 = ((bf16[32,16,768]{2,1,0:T(8,128)(2,1)}), bf16[32,16,768]{2,1,0:T(8,128)(2,1)S(1)}, u32[]{:S(2)}, u32[]{:S(2)}) async-start(bf16[32,16,768]{2,1,0:T(8,128)(2,1)} %bitcast.12), calls=%async_computation.2 | async-start | bytes 1572864 | tf_op jit(solution)/shard_map/all_to_all | solution.py:70
  35.5 35.8 %slice-start = ((s8[6291456]{0:T(1024)(128)(4,1)}), s8[4194304]{0:T(1024)(128)(4,1)S(1)}, s32[]{:S(2)}) async-start(s8[6291456]{0:T(1024)(128)(4,1)} %bitcast.24), calls=%async_computation.3 | async-start | bytes 8388608
  36.1 35.2 %slice-start.1 = ((s8[6291456]{0:T(1024)(128)(4,1)}), s8[2097152]{0:T(1024)(128)(4,1)S(1)}, s32[]{:S(2)}) async-start(s8[6291456]{0:T(1024)(128)(4,1)} %bitcast.24), calls=%async_computation.4 | async-start | bytes 4194304
  36.1 33.4 %collective-permute-start.1 = (bf16[512,768]{1,0:T(8,128)(2,1)S(1)}, bf16[512,768]{1,0:T(8,128)(2,1)S(1)}, u32[]{:S(2)}, u32[]{:S(2)}) collective-permute-start(bf16[512,768]{1,0:T(8,128)(2,1)S(1)} %collective-permute-done), channel_id=1, source_target_pairs={{0,8},{8,16},{16,24},{24,0},{1,9},{9,17},{17,25},{25,1},{2,10},{10... | collective-permute-start | bytes 2359304 | tf_op jit(solution)/shard_map/ppermute | solution.py:15
  69.6 20.8 %collective-permute-start.2 = (bf16[512,768]{1,0:T(8,128)(2,1)S(1)}, bf16[512,768]{1,0:T(8,128)(2,1)S(1)}, u32[]{:S(2)}, u32[]{:S(2)}) collective-permute-start(bf16[512,768]{1,0:T(8,128)(2,1)S(1)} %collective-permute-done.1), channel_id=1, source_target_pairs={{0,8},{8,16},{16,24},{24,0},{1,9},{9,17},{17,25},{25,1},{2,10},{10... | collective-permute-start | bytes 2359304 | tf_op jit(solution)/shard_map/ppermute | solution.py:15
  95.6 9.0 %all-to-all-start = ((f32[4,1,512]{2,1,0:T(1,128)}), f32[4,1,512]{2,1,0:T(1,128)S(1)}, u32[]{:S(2)}, u32[]{:S(2)}) async-start(f32[4,1,512]{2,1,0:T(1,128)} %copy.17), calls=%async_computation | async-start | bytes 16384 | tf_op jit(solution)/shard_map/all_to_all | solution.py:49
where the time goes:
time: 106 us; the launch traced here: 105 us
  waiting for transfers between devices  45 us (42%)
  matrix products  21.5 us (20%)
  starting transfers between devices  20.7 us (20%)
  other arithmetic  10.7 us (10%)
  local copies, waits for them, and re-layouts  4.04 us (4%)
  between operations  3.29 us (3%)
    ppermute x3, waiting for transfers between devices, shifted(): return lax.ppermute(value, axis, pairs)  40.2 us
    dot_general x4, matrix products, tile_max(): lax.dot_general(rows, index_unit, (((1,), (1,)), ((), ())), preferred_ele...  18.5 us
    all_to_all x1, starting transfers between devices, per_device(): lax.all_to_all(tagging, ('blk', 'slab'), split_axis=0, concat_axis=0, til...  7.33 us
    reduce_sum x2, other arithmetic, unit_rows(): scale = lax.rsqrt(jnp.sum(wide * wide, axis=-1, keepdims=True) + EPS)  5.6 us
    ppermute x3, starting transfers between devices, shifted(): return lax.ppermute(value, axis, pairs)  5.32 us
    all_to_all x1, waiting for transfers between devices, per_device(): lax.all_to_all(by_anchor, 'blk', split_axis=0, concat_axis=0, tiled=True)  4.73 us
    all_to_all x1, starting transfers between devices, per_device(): lax.all_to_all(payload, ('blk', 'slab'), split_axis=0, concat_axis=0, til...  4.63 us
    all_to_all x1, starting transfers between devices, per_device(): lax.all_to_all(by_anchor, 'blk', split_axis=0, concat_axis=0, tiled=True)  3.43 us
  transfers between devices with their start and end apart: 6, of which 3 were waited for; matrix products, arithmetic and copies ran while one was open for 31% of the time, Pallas kernels for 0%

commit v1 on v0

v1 whole, which is shorter than its diff:
```python
import jax
import jax.numpy as jnp
from jax import lax
from jax.sharding import PartitionSpec as P


CL_DEV = 16
EPS = 1e-06
PIECES = 2
LANES = 128


def shifted(value, axis, steps):
    count = lax.axis_size(axis)
    pairs = [(source, (source + steps) % count) for source in range(count)]
    return lax.ppermute(value, axis, pairs)


def inverse_norm(values):
    wide = values.astype(jnp.float32)
    return lax.rsqrt(jnp.sum(wide * wide, axis=-1, keepdims=True) + EPS)


def unit_rows(values):
    return (values.astype(jnp.float32) * inverse_norm(values)).astype(jnp.bfloat16)


def kept_sums(new_unit, kept_row, owner, kept_local):
    cycle = lax.axis_size("blk")
    lanes = lax.axis_size("slab")
    rows, width = new_unit.shape
    entries = kept_row.shape[0]
    pick = (kept_row[:, None] == jnp.arange(rows, dtype=jnp.int32)[None, :]).astype(jnp.bfloat16)
    picked = jnp.dot(pick, new_unit, preferred_element_type=jnp.float32).astype(jnp.bfloat16)
    picked = jnp.concatenate([picked, jnp.ones((entries, LANES), jnp.bfloat16)], axis=1)
    place = ((owner % lanes) * cycle + owner // lanes) * CL_DEV + kept_local
    spread = (jnp.arange(lanes * cycle * CL_DEV, dtype=jnp.int32)[:, None] == place[None, :]).astype(
        jnp.bfloat16
    )
    part = jnp.dot(spread, picked, preferred_element_type=jnp.float32)
    part = part.reshape(lanes, cycle * CL_DEV, width + LANES)
    part = lax.all_to_all(part, "slab", split_axis=0, concat_axis=0, tiled=True)
    part = jnp.sum(part, axis=0).astype(jnp.bfloat16)
    part = part.reshape(cycle, CL_DEV, width + LANES)
    part = lax.all_to_all(part, "blk", split_axis=0, concat_axis=0, tiled=True)
    total = jnp.sum(part.astype(jnp.float32), axis=0)
    return total[:, :width], total[:, width]


def per_device(new_rows, index_rows, pattern, kept_row, kept_owner, kept_local):
    cycle = lax.axis_size("blk")
    lanes = lax.axis_size("slab")
    here = lax.axis_index("blk")
    lane = lax.axis_index("slab")
    index_unit = unit_rows(index_rows)

    def tile_max(rows):
        scores = lax.dot_general(
            rows, index_unit, (((1,), (1,)), ((), ())), preferred_element_type=jnp.float32
        )
        return jnp.max(scores, axis=1)

    piece = new_rows.shape[0] // PIECES
    moving = [new_rows[i * piece : (i + 1) * piece] for i in range(PIECES)]
    home = [tile_max(new_rows)]
    for step in range(1, cycle):
        tops = []
        for i in range(PIECES):
            moving[i] = shifted(moving[i], "blk", 1)
            tops.append(tile_max(moving[i]))
        home.append(shifted(jnp.concatenate(tops), "blk", -step))
    scale = lax.optimization_barrier(inverse_norm(new_rows))
    sums, counts = kept_sums(
        (new_rows.astype(jnp.float32) * scale).astype(jnp.bfloat16),
        kept_row,
        kept_owner[:, 0],
        kept_local,
    )
    marks = lax.dynamic_slice_in_dim(pattern, here * lanes + lane, 1, axis=0)[0]
    best = jnp.full((new_rows.shape[0],), -2.0, jnp.float32)
    for step in range(cycle):
        live = marks[(here + step) % cycle] > 0
        best = jnp.maximum(best, jnp.where(live, home[step] * scale[:, 0], jnp.float32(-2.0)))
    return best, sums, counts


def solution(mesh):
    placed = (
        P(("blk", "slab"), None),
        P("blk", None),
        P(),
        P(("blk", "slab")),
        P(("blk", "slab"), None),
        P(("blk", "slab")),
    )
    return jax.shard_map(
        per_device,
        mesh=mesh,
        in_specs=placed,
        out_specs=(P(("blk", "slab")), P(("blk", "slab"), None), P(("blk", "slab"))),
        check_vma=False,
    )
```

time: 106 us -> 88.7 us (0.84)
  waiting for transfers between devices: 45 us -> 28.3 us
  matrix products: 21.5 us -> 28 us
  other arithmetic: 10.7 us -> 7.54 us
  starting transfers between devices: 20.7 us -> 17.7 us
    ppermute x3 -> x9, waiting for transfers between devices: 40.2 us -> 23.1 us  [shifted(): return lax.ppermute(value, axis, pairs)]
    all_to_all x3 -> x2, starting transfers between devices: 15.4 us -> 8.74 us  [the longest x1 5.02 us: kept_sums(): part = lax.all_to_all(part, 'blk', split_axis=0, concat_axis=0, tiled=True)]
    dot_general x4 -> x7, matrix products: 18.5 us -> 24.6 us  [tile_max(): lax.dot_general(rows, index_unit, (((1,), (1,)), ((), ())), preferred_ele...]
    ppermute x3 -> x9, starting transfers between devices: 5.32 us -> 8.95 us  [shifted(): return lax.ppermute(value, axis, pairs)]
    slice x0 -> x3, local copies, waits for them, and re-layouts: none -> 2.42 us  [the longest x2 1.25 us: kept_sums(): return (total[:, :width], total[:, width])]
    gather x2 -> x0, local copies, waits for them, and re-layouts: 1.76 us -> none  [the longest x1 1.19 us: per_device(): picked = new_unit[kept_row]]
    convert_element_type x1 -> x0, other arithmetic: 1.33 us -> none  [unit_rows(): return (wide * scale).astype(jnp.bfloat16)]
    all_to_all x3 -> x2, waiting for transfers between devices: 4.74 us -> 5.27 us  [the longest x1 5.27 us: kept_sums(): part = lax.all_to_all(part, 'blk', split_axis=0, concat_axis=0, tiled=True)]
  transfers between devices with their start and end apart: 6 -> 11, of which waited for: 3 -> 4; matrix products, arithmetic and copies ran while one was open for 31% -> 41% of each run, Pallas kernels for 0% -> 0%
where the time goes in v1:
time: 88.7 us; the launch traced here: 88.2 us
  waiting for transfers between devices  28.3 us (32%)
  matrix products  28 us (32%)
  starting transfers between devices  17.7 us (20%)
  other arithmetic  7.54 us (9%)
  between operations  3.59 us (4%)
  local copies, waits for them, and re-layouts  3.12 us (4%)
    dot_general x7, matrix products, tile_max(): lax.dot_general(rows, index_unit, (((1,), (1,)), ((), ())), preferred_ele...  24.6 us
    ppermute x9, waiting for transfers between devices, shifted(): return lax.ppermute(value, axis, pairs)  23.1 us
    ppermute x9, starting transfers between devices, shifted(): return lax.ppermute(value, axis, pairs)  8.95 us
    reduce_sum x2, other arithmetic, inverse_norm(): return lax.rsqrt(jnp.sum(wide * wide, axis=-1, keepdims=True) + EPS)  5.44 us
    all_to_all x1, waiting for transfers between devices, kept_sums(): part = lax.all_to_all(part, 'blk', split_axis=0, concat_axis=0, tiled=True)  5.27 us
    all_to_all x1, starting transfers between devices, kept_sums(): part = lax.all_to_all(part, 'blk', split_axis=0, concat_axis=0, tiled=True)  5.02 us
    all_to_all x1, starting transfers between devices, kept_sums(): part = lax.all_to_all(part, 'slab', split_axis=0, concat_axis=0, tiled=True)  3.72 us
  transfers between devices with their start and end apart: 11, of which 4 were waited for; matrix products, arithmetic and copies ran while one was open for 41% of the time, Pallas kernels for 0%

profile of v1, /device:TPU:0, one launch (start us, length us, event | category | flops | bytes accessed | tf_op | source)
XLA Modules:
  0.0 88.2 jit_solution(6209196944400093445)
XLA Ops:
  0.6 1.2 %fusion.20 = (bf16[256,768]{1,0:T(8,128)(2,1)S(1)}, bf16[256,768]{1,0:T(8,128)(2,1)S(1)}) fusion(bf16[512,768]{1,0:T(8,128)(2,1)} %param.6), kind=kLoop, calls=%fused_computation.40 | loop fusion | bytes 1572864 | tf_op jit(solution)/shard_map/slice | solution.py:64
  1.8 3.1 %collective-permute-start = (bf16[256,768]{1,0:T(8,128)(2,1)S(1)}, bf16[256,768]{1,0:T(8,128)(2,1)}, u32[]{:S(2)}, u32[]{:S(2)}) collective-permute-start(bf16[256,768]{1,0:T(8,128)(2,1)S(1)} %get-tuple-element.3), channel_id=1, source_target_pairs={{0,8},{8,16},{16,24},{24,0},{1,9},{9,17},{17,25},{25,1},{2,10},{10... | collective-permute-start | bytes 1179656 | tf_op jit(solution)/shard_map/ppermute | solution.py:16
  4.9 1.6 %collective-permute-start.1 = (bf16[256,768]{1,0:T(8,128)(2,1)S(1)}, bf16[256,768]{1,0:T(8,128)(2,1)}, u32[]{:S(2)}, u32[]{:S(2)}) collective-permute-start(bf16[256,768]{1,0:T(8,128)(2,1)S(1)} %get-tuple-element.4), channel_id=1, source_target_pairs={{0,8},{8,16},{16,24},{24,0},{1,9},{9,17},{17,25},{25,1},{2,10},{10... | collective-permute-start | bytes 1179656 | tf_op jit(solution)/shard_map/ppermute | solution.py:16
  6.5 1.4 %fusion.2 = f32[512]{0:T(512)S(1)} fusion(bf16[512,768]{1,0:T(8,128)(2,1)} %param.6), kind=kLoop, calls=%fused_computation.13 | loop fusion | flops 1179136 | bytes 788480 | tf_op jit(solution)/shard_map/reduce_sum | solution.py:21
  7.9 0.7 multiply_add_fusion
  8.6 1.7 %convolution_convert_fusion = bf16[256,768]{1,0:T(8,128)(2,1)S(1)} fusion(bf16[512,768]{1,0:T(8,128)(2,1)} %param.6, f32[512]{0:T(512)S(1)} %add_rsqrt_fusion.1, s32[256]{0:T(256)} %param.9), kind=kOutput, calls=%fused_computation.15 | convolution fusion | flops 202833920 | bytes 1182720 | tf_op jit(solution)/shard_map/dot_general | solution.py:34
  10.3 1.7 %fusion.6 = f32[512,896]{1,0:T(8,128)} fusion(bf16[256,768]{1,0:T(8,128)(2,1)S(1)} %convolution_convert_fusion, s32[256]{0:T(256)S(1)} %multiply_add_fusion), kind=kOutput, calls=%fused_computation.19 | convolution fusion | flops 235012096 | bytes 2229248 | tf_op jit(solution)/shard_map/dot_general | solution.py:40
  12.0 3.7 %all-to-all-start = ((f32[8,64,896]{2,1,0:T(8,128)}), f32[8,64,896]{2,1,0:T(8,128)S(1)}, u32[]{:S(2)}, u32[]{:S(2)}) async-start(f32[8,64,896]{2,1,0:T(8,128)} %bitcast.16), calls=%async_computation | async-start | bytes 3670016 | tf_op jit(solution)/shard_map/all_to_all | solution.py:42
  15.7 4.1 %fusion = f32[4096]{0:T(1024)S(1)} fusion(bf16[4096,768]{1,0:T(8,128)(2,1)} %param.7), kind=kLoop, calls=%fused_computation.2 | loop fusion | flops 9433088 | bytes 6307840 | tf_op jit(solution)/shard_map/reduce_sum | solution.py:21
  19.8 6.3 %convolution_reduce_fusion = f32[512]{0:T(512)S(1)} fusion(bf16[512,768]{1,0:T(8,128)(2,1)S(1)} %copy-done, bf16[4096,768]{1,0:T(8,128)(2,1)} %param.7, f32[4096]{0:T(1024)S(1)} %add_rsqrt_fusion), kind=kOutput, calls=%fused_computation.4 | convolution fusion | flops 3232759296 | bytes 7096320 | tf_op jit(solution)/shard_map/dot_general | solution.py:58
  26.1 1.6 %collective-permute-start.3 = (bf16[256,768]{1,0:T(8,128)(2,1)}, bf16[256,768]{1,0:T(8,128)(2,1)S(1)}, u32[]{:S(2)}, u32[]{:S(2)}) collective-permute-start(bf16[256,768]{1,0:T(8,128)(2,1)} %collective-permute-done), channel_id=1, source_target_pairs={{0,8},{8,16},{16,24},{24,0},{1,9},{9,17},{17,25},{25,1},{2,10},{10... | collective-permute-start | bytes 1179656 | tf_op jit(solution)/shard_map/ppermute | solution.py:16
  27.8 4.8 %convolution_reduce_fusion.6 = f32[256]{0:T(256)S(1)} fusion(bf16[256,768]{1,0:T(8,128)(2,1)} %collective-permute-done, bf16[4096,768]{1,0:T(8,128)(2,1)} %param.7, f32[4096]{0:T(1024)S(1)} %add_rsqrt_fusion), kind=kOutput, calls=%fused_computation.12 | convolution fusion | flops 1621098240 | bytes 6702080 | tf_op jit(solution)/shard_map/dot_general | solution.py:58
  32.6 4.8 %convolution_reduce_fusion.5 = f32[256]{0:T(256)S(1)} fusion(bf16[256,768]{1,0:T(8,128)(2,1)} %collective-permute-done.1, bf16[4096,768]{1,0:T(8,128)(2,1)} %param.7, f32[4096]{0:T(1024)S(1)} %add_rsqrt_fusion), kind=kOutput, calls=%fused_computation.11 | convolution fusion | flops 1621098240 | bytes 6702080 | tf_op jit(solution)/shard_map/dot_general | solution.py:58
  37.5 2.3 %collective-permute-start.2 = (f32[512]{0:T(512)S(1)}, f32[512]{0:T(512)S(1)}, u32[]{:S(2)}, u32[]{:S(2)}) collective-permute-start(f32[512]{0:T(512)S(1)} %pad_maximum_fusion), channel_id=1, source_target_pairs={{0,24},{8,0},{16,8},{24,16},{1,25},{9,1},{17,9},{25,17},{2,26},{10... | collective-permute-start | bytes 6152 | tf_op jit(solution)/shard_map/ppermute | solution.py:16
  39.8 2.2 %convolution_reduce_fusion.4 = f32[256]{0:T(256)S(1)} fusion(bf16[256,768]{1,0:T(8,128)(2,1)S(1)} %collective-permute-done.3, bf16[4096,768]{1,0:T(8,128)(2,1)S(1)} %bitcast.18, f32[4096]{0:T(1024)S(1)} %add_rsqrt_fusion), kind=kOutput, calls=%fused_computation.10 | convolution fusion | flops 1621098240 | bytes 6702080 | tf_op jit(solution)/shard_map/dot_general | solution.py:58
  42.0 11.8 %collective-permute-done.4 = bf16[256,768]{1,0:T(8,128)(2,1)S(1)} collective-permute-done((bf16[256,768]{1,0:T(8,128)(2,1)}, bf16[256,768]{1,0:T(8,128)(2,1)S(1)}, u32[]{:S(2)}, u32[]{:S(2)}) %collective-permute-start.4) | collective-permute-done | bytes 393248 | tf_op jit(solution)/shard_map/ppermute | solution.py:16
  53.8 2.2 %convolution_reduce_fusion.3 = f32[256]{0:T(256)S(1)} fusion(bf16[256,768]{1,0:T(8,128)(2,1)S(1)} %collective-permute-done.4, bf16[4096,768]{1,0:T(8,128)(2,1)S(1)} %bitcast.18, f32[4096]{0:T(1024)S(1)} %add_rsqrt_fusion), kind=kOutput, calls=%fused_computation.9 | convolution fusion | flops 1621098240 | bytes 6702080 | tf_op jit(solution)/shard_map/dot_general | solution.py:58
  56.2 6.0 %collective-permute-done.6 = bf16[256,768]{1,0:T(8,128)(2,1)S(1)} collective-permute-done((bf16[256,768]{1,0:T(8,128)(2,1)S(1)}, bf16[256,768]{1,0:T(8,128)(2,1)S(1)}, u32[]{:S(2)}, u32[]{:S(2)}) %collective-permute-start.6) | collective-permute-done | bytes 393248 | tf_op jit(solution)/shard_map/ppermute | solution.py:16
  62.2 2.2 %convolution_reduce_fusion.2 = f32[256]{0:T(256)S(1)} fusion(bf16[256,768]{1,0:T(8,128)(2,1)S(1)} %collective-permute-done.6, bf16[4096,768]{1,0:T(8,128)(2,1)S(1)} %bitcast.18, f32[4096]{0:T(1024)S(1)} %add_rsqrt_fusion), kind=kOutput, calls=%fused_computation.8 | convolution fusion | flops 1621098240 | bytes 6702080 | tf_op jit(solution)/shard_map/dot_general | solution.py:58
  64.4 5.3 %collective-permute-done.7 = bf16[256,768]{1,0:T(8,128)(2,1)S(1)} collective-permute-done((bf16[256,768]{1,0:T(8,128)(2,1)S(1)}, bf16[256,768]{1,0:T(8,128)(2,1)S(1)}, u32[]{:S(2)}, u32[]{:S(2)}) %collective-permute-start.7) | collective-permute-done | bytes 393248 | tf_op jit(solution)/shard_map/ppermute | solution.py:16
  69.7 2.2 %convolution_reduce_fusion.1 = f32[256]{0:T(256)S(1)} fusion(bf16[256,768]{1,0:T(8,128)(2,1)S(1)} %collective-permute-done.7, bf16[4096,768]{1,0:T(8,128)(2,1)S(1)} %bitcast.18, f32[4096]{0:T(1024)S(1)} %add_rsqrt_fusion), kind=kOutput, calls=%fused_computation.7 | convolution fusion | flops 1621098240 | bytes 6702080 | tf_op jit(solution)/shard_map/dot_general | solution.py:58
  75.3 0.7 reduce_sum.38
  76.1 5.0 %all-to-all-start.1 = ((bf16[4,16,896]{2,1,0:T(8,128)(2,1)}), bf16[4,16,896]{2,1,0:T(8,128)(2,1)S(1)}, u32[]{:S(2)}, u32[]{:S(2)}) async-start(bf16[4,16,896]{2,1,0:T(8,128)(2,1)} %bitcast.8), calls=%async_computation.1 | async-start | bytes 229376 | tf_op jit(solution)/shard_map/all_to_all | solution.py:45
  81.7 5.3 %all-to-all-done.1 = bf16[4,16,896]{2,1,0:T(8,128)(2,1)S(1)} async-done(((bf16[4,16,896]{2,1,0:T(8,128)(2,1)}), bf16[4,16,896]{2,1,0:T(8,128)(2,1)S(1)}, u32[]{:S(2)}, u32[]{:S(2)}) %all-to-all-start.1) | async-done | bytes 114720 | tf_op jit(solution)/shard_map/all_to_all | solution.py:45
  (31 shorter events, 3.0 us)
Async XLA Ops:
  1.8 24.3 %collective-permute-start = (bf16[256,768]{1,0:T(8,128)(2,1)S(1)}, bf16[256,768]{1,0:T(8,128)(2,1)}, u32[]{:S(2)}, u32[]{:S(2)}) collective-permute-start(bf16[256,768]{1,0:T(8,128)(2,1)S(1)} %get-tuple-element.3), channel_id=1, source_target_pairs={{0,8},{8,16},{16,24},{24,0},{1,9},{9,17},{17,25},{25,1},{2,10},{10... | collective-permute-start | bytes 1179656 | tf_op jit(solution)/shard_map/ppermute | solution.py:16
  4.9 27.7 %collective-permute-start.1 = (bf16[256,768]{1,0:T(8,128)(2,1)S(1)}, bf16[256,768]{1,0:T(8,128)(2,1)}, u32[]{:S(2)}, u32[]{:S(2)}) collective-permute-start(bf16[256,768]{1,0:T(8,128)(2,1)S(1)} %get-tuple-element.4), channel_id=1, source_target_pairs={{0,8},{8,16},{16,24},{24,0},{1,9},{9,17},{17,25},{25,1},{2,10},{10... | collective-permute-start | bytes 1179656 | tf_op jit(solution)/shard_map/ppermute | solution.py:16
  10.2 9.5 %copy-start = (bf16[512,768]{1,0:T(8,128)(2,1)S(1)}, bf16[512,768]{1,0:T(8,128)(2,1)}, u32[]{:S(2)}) copy-start(bf16[512,768]{1,0:T(8,128)(2,1)} %param.6) | copy-start | bytes 2359300
  12.0 63.4 %all-to-all-start = ((f32[8,64,896]{2,1,0:T(8,128)}), f32[8,64,896]{2,1,0:T(8,128)S(1)}, u32[]{:S(2)}, u32[]{:S(2)}) async-start(f32[8,64,896]{2,1,0:T(8,128)} %bitcast.16), calls=%async_computation | async-start | bytes 3670016 | tf_op jit(solution)/shard_map/all_to_all | solution.py:42
  26.1 13.6 %collective-permute-start.3 = (bf16[256,768]{1,0:T(8,128)(2,1)}, bf16[256,768]{1,0:T(8,128)(2,1)S(1)}, u32[]{:S(2)}, u32[]{:S(2)}) collective-permute-start(bf16[256,768]{1,0:T(8,128)(2,1)} %collective-permute-done), channel_id=1, source_target_pairs={{0,8},{8,16},{16,24},{24,0},{1,9},{9,17},{17,25},{25,1},{2,10},{10... | collective-permute-start | bytes 1179656 | tf_op jit(solution)/shard_map/ppermute | solution.py:16
  27.8 12.0 %slice-start = ((s8[6291456]{0:T(1024)(128)(4,1)}), s8[4194304]{0:T(1024)(128)(4,1)S(1)}, s32[]{:S(2)}) async-start(s8[6291456]{0:T(1024)(128)(4,1)} %bitcast.17), calls=%async_computation.2 | async-start | bytes 8388608
  32.6 7.2 %slice-start.1 = ((s8[6291456]{0:T(1024)(128)(4,1)}), s8[2097152]{0:T(1024)(128)(4,1)S(1)}, s32[]{:S(2)}) async-start(s8[6291456]{0:T(1024)(128)(4,1)} %bitcast.17), calls=%async_computation.3 | async-start | bytes 4194304
  37.5 43.6 %collective-permute-start.2 = (f32[512]{0:T(512)S(1)}, f32[512]{0:T(512)S(1)}, u32[]{:S(2)}, u32[]{:S(2)}) collective-permute-start(f32[512]{0:T(512)S(1)} %pad_maximum_fusion), channel_id=1, source_target_pairs={{0,24},{8,0},{16,8},{24,16},{1,25},{9,1},{17,9},{25,17},{2,26},{10... | collective-permute-start | bytes 6152 | tf_op jit(solution)/shard_map/ppermute | solution.py:16
  39.8 14.0 %collective-permute-start.4 = (bf16[256,768]{1,0:T(8,128)(2,1)}, bf16[256,768]{1,0:T(8,128)(2,1)S(1)}, u32[]{:S(2)}, u32[]{:S(2)}) collective-permute-start(bf16[256,768]{1,0:T(8,128)(2,1)} %collective-permute-done.1), channel_id=1, source_target_pairs={{0,8},{8,16},{16,24},{24,0},{1,9},{9,17},{17,25},{25,1},{2,10},{10... | collective-permute-start | bytes 1179656 | tf_op jit(solution)/shard_map/ppermute | solution.py:16
  39.8 22.5 %collective-permute-start.6 = (bf16[256,768]{1,0:T(8,128)(2,1)S(1)}, bf16[256,768]{1,0:T(8,128)(2,1)S(1)}, u32[]{:S(2)}, u32[]{:S(2)}) collective-permute-start(bf16[256,768]{1,0:T(8,128)(2,1)S(1)} %collective-permute-done.3), channel_id=1, source_target_pairs={{0,8},{8,16},{16,24},{24,0},{1,9},{9,17},{17,25},{25,1},{2,10},{10... | collective-permute-start | bytes 1179656 | tf_op jit(solution)/shard_map/ppermute | solution.py:16
  56.0 25.1 %collective-permute-start.5 = (f32[512]{0:T(512)S(1)}, f32[512]{0:T(512)S(1)}, u32[]{:S(2)}, u32[]{:S(2)}) collective-permute-start(f32[512]{0:T(512)S(1)} %pad_maximum_fusion.1), channel_id=1, source_target_pairs={{0,16},{8,24},{16,0},{24,8},{1,17},{9,25},{17,1},{25,9},{2,18},{10... | collective-permute-start | bytes 6152 | tf_op jit(solution)/shard_map/ppermute | solution.py:16
  56.0 13.7 %collective-permute-start.7 = (bf16[256,768]{1,0:T(8,128)(2,1)S(1)}, bf16[256,768]{1,0:T(8,128)(2,1)S(1)}, u32[]{:S(2)}, u32[]{:S(2)}) collective-permute-start(bf16[256,768]{1,0:T(8,128)(2,1)S(1)} %collective-permute-done.4), channel_id=1, source_target_pairs={{0,8},{8,16},{16,24},{24,0},{1,9},{9,17},{17,25},{25,1},{2,10},{10... | collective-permute-start | bytes 1179656 | tf_op jit(solution)/shard_map/ppermute | solution.py:16
  64.4 7.6 %copy-start.1 = (s32[32,4]{0,1:T(4,128)S(1)}, s32[32,4]{0,1:T(4,128)}, u32[]{:S(2)}) copy-start(s32[32,4]{0,1:T(4,128)} %param.8) | copy-start | bytes 1540
  71.9 9.2 %collective-permute-start.8 = (f32[512]{0:T(512)S(1)}, f32[512]{0:T(512)S(1)}, u32[]{:S(2)}, u32[]{:S(2)}) collective-permute-start(f32[512]{0:T(512)S(1)} %pad_maximum_fusion.2), channel_id=1, source_target_pairs={{0,8},{8,16},{16,24},{24,0},{1,9},{9,17},{17,25},{25,1},{2,10},{10... | collective-permute-start | bytes 6152 | tf_op jit(solution)/shard_map/ppermute | solution.py:16
  76.1 10.9 %all-to-all-start.1 = ((bf16[4,16,896]{2,1,0:T(8,128)(2,1)}), bf16[4,16,896]{2,1,0:T(8,128)(2,1)S(1)}, u32[]{:S(2)}, u32[]{:S(2)}) async-start(bf16[4,16,896]{2,1,0:T(8,128)(2,1)} %bitcast.8), calls=%async_computation.1 | async-start | bytes 229376 | tf_op jit(solution)/shard_map/all_to_all | solution.py:45

commit v2 on v1

v2 whole, which is shorter than its diff:
```python
import jax
import jax.numpy as jnp
from jax import lax
from jax.sharding import PartitionSpec as P


CL_DEV = 16
EPS = 1e-06
PIECES = 2
LANES = 128


def shifted(value, axis, steps):
    count = lax.axis_size(axis)
    pairs = [(source, (source + steps) % count) for source in range(count)]
    return lax.ppermute(value, axis, pairs)


def swapped(value, axis, bit):
    count = lax.axis_size(axis)
    return lax.ppermute(value, axis, [(source, source ^ bit) for source in range(count)])


def inverse_norm(values):
    wide = values.astype(jnp.float32)
    return lax.rsqrt(jnp.sum(wide * wide, axis=-1, keepdims=True) + EPS)


def halvings(lanes):
    return lanes.bit_length() - 1


def kept_sums(new_unit, kept_row, owner, kept_local):
    cycle = lax.axis_size("blk")
    lanes = lax.axis_size("slab")
    here = lax.axis_index("blk")
    lane = lax.axis_index("slab")
    rows, width = new_unit.shape
    entries = kept_row.shape[0]
    levels = halvings(lanes)
    pick = (kept_row[:, None] == jnp.arange(rows, dtype=jnp.int32)[None, :]).astype(jnp.bfloat16)
    picked = jnp.dot(pick, new_unit, preferred_element_type=jnp.float32).astype(jnp.bfloat16)
    picked = jnp.concatenate([picked, jnp.ones((entries, LANES), jnp.bfloat16)], axis=1)
    apart = (owner % lanes) ^ lane
    mirrored = jnp.zeros_like(apart)
    for level in range(levels):
        mirrored = mirrored * 2 + ((apart >> level) & 1)
    ahead = (owner // lanes - here) % cycle
    place = (mirrored * cycle + ahead) * CL_DEV + kept_local
    total = lanes * cycle * CL_DEV
    spread = (jnp.arange(total, dtype=jnp.int32)[:, None] == place[None, :]).astype(jnp.bfloat16)
    half = total // 2
    keep = jnp.dot(spread[:half], picked, preferred_element_type=jnp.float32)
    send = jnp.dot(spread[half:], picked, preferred_element_type=jnp.float32)
    for level in range(levels):
        got = swapped(send, "slab", 1 << level)
        whole = keep + got
        half = whole.shape[0] // 2
        keep, send = whole[:half], whole[half:]
    parts = [whole[:CL_DEV]]
    for step in range(1, cycle):
        part = whole[step * CL_DEV : (step + 1) * CL_DEV].astype(jnp.bfloat16)
        parts.append(shifted(part, "blk", step))
    sums = parts[0]
    for part in parts[1:]:
        sums = sums + part.astype(jnp.float32)
    return sums[:, :width], sums[:, width]


def per_device(new_rows, index_rows, pattern, kept_row, kept_owner, kept_local):
    cycle = lax.axis_size("blk")
    lanes = lax.axis_size("slab")
    here = lax.axis_index("blk")
    lane = lax.axis_index("slab")
    rows = new_rows.shape[0]
    index_scale = inverse_norm(index_rows)[:, 0]

    def tile_max(block):
        scores = lax.dot_general(
            block, index_rows, (((1,), (1,)), ((), ())), preferred_element_type=jnp.float32
        )
        return jnp.max(scores * index_scale[None, :], axis=1)

    piece = rows // PIECES
    moving = [new_rows[:piece]]
    kept_apart = lax.optimization_barrier(new_rows)
    moving += [kept_apart[i * piece : (i + 1) * piece] for i in range(1, PIECES)]
    home = [tile_max(new_rows)]
    for step in range(1, cycle):
        tops = []
        for i in range(PIECES):
            moving[i] = shifted(moving[i], "blk", 1)
            tops.append(tile_max(moving[i]))
        home.append(shifted(jnp.concatenate(tops), "blk", -step))
    scale = lax.optimization_barrier(inverse_norm(new_rows))
    sums, counts = kept_sums(
        (new_rows.astype(jnp.float32) * scale).astype(jnp.bfloat16),
        kept_row,
        kept_owner[:, 0],
        kept_local,
    )
    wanted = (here + jnp.arange(cycle, dtype=jnp.int32)) % cycle
    mine = (jnp.arange(cycle * lanes, dtype=jnp.int32) == here * lanes + lane)[None, :, None] & (
        jnp.arange(cycle, dtype=jnp.int32)[None, None, :] == wanted[:, None, None]
    )
    live = jnp.max(jnp.where(mine, pattern[None], 0), axis=(1, 2))
    live = lax.optimization_barrier(jnp.broadcast_to(live[:, None], (cycle, rows)))

    def masked(step):
        return jnp.where(live[step] > 0, home[step] * scale[:, 0], jnp.float32(-2.0))

    best = masked(0)
    for step in range(1, cycle - 1):
        best = jnp.maximum(best, masked(step))
    best = lax.optimization_barrier(best)
    best = jnp.maximum(best, masked(cycle - 1))
    return best, sums, counts


def solution(mesh):
    placed = (
        P(("blk", "slab"), None),
        P("blk", None),
        P(),
        P(("blk", "slab")),
        P(("blk", "slab"), None),
        P(("blk", "slab")),
    )
    return jax.shard_map(
        per_device,
        mesh=mesh,
        in_specs=placed,
        out_specs=(P(("blk", "slab")), P(("blk", "slab"), None), P(("blk", "slab"))),
        check_vma=False,
    )
```

time: 88.7 us -> 78.8 us (0.89)
  matrix products: 28 us -> 19.6 us
  between operations: 3.59 us -> 0.85 us
  waiting for transfers between devices: 28.3 us -> 26 us
  starting transfers between devices: 17.7 us -> 19.8 us
  local copies, waits for them, and re-layouts: 3.12 us -> 4.58 us
    all_to_all x2 -> x0, starting transfers between devices: 8.74 us -> none  [the longest x1 5.02 us: kept_sums(): part = lax.all_to_all(part, 'blk', split_axis=0, concat_axis=0, tiled=True)]
    dot_general x8 -> x9, matrix products: 26.3 us -> 18 us  [the longest x7 17.3 us: tile_max(): lax.dot_general(block, index_rows, (((1,), (1,)), ((), ())), preferred_el...]
    ppermute x9 -> x12, starting transfers between devices: 8.95 us -> 16.6 us  [shifted(): return lax.ppermute(value, axis, pairs)]
    all_to_all x2 -> x0, waiting for transfers between devices: 5.27 us -> none  [the longest x1 5.27 us: kept_sums(): part = lax.all_to_all(part, 'blk', split_axis=0, concat_axis=0, tiled=True)]
    ppermute x0 -> x3, starting transfers between devices: none -> 3.21 us  [swapped(): lax.ppermute(value, axis, [(source, source ^ bit) for source in range(cou...]
    ppermute x9 -> x12, waiting for transfers between devices: 23.1 us -> 26 us  [shifted(): return lax.ppermute(value, axis, pairs)]
    slice x3 -> x7, local copies, waits for them, and re-layouts: 2.42 us -> 4.17 us  [the longest x1 1.84 us: per_device(): moving = [new_rows[:piece]]]
  transfers between devices with their start and end apart: 11 -> 15, of which waited for: 4 -> 7; matrix products, arithmetic and copies ran while one was open for 41% -> 36% of each run, Pallas kernels for 0% -> 0%
where the time goes in v2:
time: 78.8 us; the launch traced here: 78.5 us
  waiting for transfers between devices  26 us (33%)
  starting transfers between devices  19.8 us (25%)
  matrix products  19.6 us (25%)
  other arithmetic  7.5 us (10%)
  local copies, waits for them, and re-layouts  4.58 us (6%)
  between operations  0.85 us (1%)
    ppermute x12, waiting for transfers between devices, shifted(): return lax.ppermute(value, axis, pairs)  26 us
    dot_general x7, matrix products, tile_max(): lax.dot_general(block, index_rows, (((1,), (1,)), ((), ())), preferred_el...  17.3 us
    ppermute x12, starting transfers between devices, shifted(): return lax.ppermute(value, axis, pairs)  16.6 us
    reduce_sum x2, other arithmetic, inverse_norm(): return lax.rsqrt(jnp.sum(wide * wide, axis=-1, keepdims=True) + EPS)  5.6 us
    ppermute x3, starting transfers between devices, swapped(): lax.ppermute(value, axis, [(source, source ^ bit) for source in range(cou...  3.21 us
    slice x1, local copies, waits for them, and re-layouts, per_device(): moving = [new_rows[:piece]]  1.84 us
    dot_general x1, matrix products, kept_sums(): jnp.dot(pick, new_unit, preferred_element_type=jnp.float32)  1.67 us
  transfers between devices with their start and end apart: 15, of which 7 were waited for; matrix products, arithmetic and copies ran while one was open for 36% of the time, Pallas kernels for 0%

profile of v2, /device:TPU:0, one launch (start us, length us, event | category | flops | bytes accessed | tf_op | source)
XLA Modules:
  0.0 78.5 jit_solution(9017721433205933334)
XLA Ops:
  0.6 1.8 %slice.59 = bf16[256,768]{1,0:T(8,128)(2,1)} slice(bf16[512,768]{1,0:T(8,128)(2,1)} %param.6), slice={[0:256], [0:768]} | slice | bytes 786432 | tf_op jit(solution)/shard_map/slice | solution.py:85
  2.5 3.1 %collective-permute-start = (bf16[256,768]{1,0:T(8,128)(2,1)}, bf16[256,768]{1,0:T(8,128)(2,1)}, u32[]{:S(2)}, u32[]{:S(2)}) collective-permute-start(bf16[256,768]{1,0:T(8,128)(2,1)} %slice.59), channel_id=1, source_target_pairs={{0,8},{8,16},{16,24},{24,0},{1,9},{9,17},{17,25},{25,1},{2,10},{10... | collective-permute-start | bytes 1179656 | tf_op jit(solution)/shard_map/ppermute | solution.py:16
  6.6 1.6 %collective-permute-start.1 = (bf16[256,768]{1,0:T(8,128)(2,1)S(1)}, bf16[256,768]{1,0:T(8,128)(2,1)}, u32[]{:S(2)}, u32[]{:S(2)}) collective-permute-start(bf16[256,768]{1,0:T(8,128)(2,1)S(1)} %slice.77), channel_id=1, source_target_pairs={{0,8},{8,16},{16,24},{24,0},{1,9},{9,17},{17,25},{25,1},{2,10},{10... | collective-permute-start | bytes 1179656 | tf_op jit(solution)/shard_map/ppermute | solution.py:16
  10.4 1.7 %convolution_convert_fusion = bf16[256,768]{1,0:T(8,128)(2,1)S(1)} fusion(bf16[512,768]{1,0:T(8,128)(2,1)} %param.6, f32[512]{0:T(512)S(1)} %add_rsqrt_fusion.1, s32[256]{0:T(256)} %param.9), kind=kOutput, calls=%fused_computation.19 | convolution fusion | flops 202833920 | bytes 1182720 | tf_op jit(solution)/shard_map/dot_general | solution.py:42
  12.5 4.2 %multiply_reduce_fusion = f32[4096]{0:T(1024)S(1)} fusion(bf16[4096,768]{1,0:T(8,128)(2,1)} %param.7), kind=kLoop, calls=%fused_computation | loop fusion | flops 9433088 | bytes 6307840 | tf_op jit(solution)/shard_map/reduce_sum | solution.py:26
  17.1 3.8 %multiply_reduce_fusion.1 = f32[512]{0:T(512)S(1)} fusion(bf16[512,768]{1,0:T(8,128)(2,1)S(1)} %copy-done.1, bf16[4096,768]{1,0:T(8,128)(2,1)S(1)} %copy-done, f32[4096]{0:T(1024)S(1)} %add_rsqrt_fusion), kind=kOutput, calls=%fused_computation.1 | convolution fusion | flops 3225419264 | bytes 7096320 | tf_op jit(solution)/shard_map/dot_general | solution.py:79
  21.3 1.6 %collective-permute-start.3 = (bf16[256,768]{1,0:T(8,128)(2,1)}, bf16[256,768]{1,0:T(8,128)(2,1)S(1)}, u32[]{:S(2)}, u32[]{:S(2)}) collective-permute-start(bf16[256,768]{1,0:T(8,128)(2,1)} %collective-permute-done), channel_id=1, source_target_pairs={{0,8},{8,16},{16,24},{24,0},{1,9},{9,17},{17,25},{25,1},{2,10},{10... | collective-permute-start | bytes 1179656 | tf_op jit(solution)/shard_map/ppermute | solution.py:16
  22.9 2.9 %fusion = f32[256]{0:T(256)S(1)} fusion(f32[4096]{0:T(1024)S(1)} %add_rsqrt_fusion, bf16[256,768]{1,0:T(8,128)(2,1)} %collective-permute-done, bf16[4096,768]{1,0:T(8,128)(2,1)S(1)} %copy-done), kind=kOutput, calls=%fused_computation.10 | convolution fusion | flops 1612709632 | bytes 6702080 | tf_op jit(solution)/shard_map/dot_general | solution.py:79
  25.8 2.9 %fusion.1 = f32[256]{0:T(256)S(1)} fusion(f32[4096]{0:T(1024)S(1)} %add_rsqrt_fusion, bf16[256,768]{1,0:T(8,128)(2,1)} %collective-permute-done.1, bf16[4096,768]{1,0:T(8,128)(2,1)S(1)} %copy-done), kind=kOutput, calls=%fused_computation.11 | convolution fusion | flops 1612709632 | bytes 6702080 | tf_op jit(solution)/shard_map/dot_general | solution.py:79
  28.7 2.3 %collective-permute-start.2 = (f32[512]{0:T(512)S(1)}, f32[512]{0:T(512)S(1)}, u32[]{:S(2)}, u32[]{:S(2)}) collective-permute-start(f32[512]{0:T(512)S(1)} %pad_maximum_fusion), channel_id=1, source_target_pairs={{0,24},{8,0},{16,8},{24,16},{1,25},{9,1},{17,9},{25,17},{2,26},{10... | collective-permute-start | bytes 6152 | tf_op jit(solution)/shard_map/ppermute | solution.py:16
  31.1 3.8 %collective-permute-done.3 = bf16[256,768]{1,0:T(8,128)(2,1)S(1)} collective-permute-done((bf16[256,768]{1,0:T(8,128)(2,1)}, bf16[256,768]{1,0:T(8,128)(2,1)S(1)}, u32[]{:S(2)}, u32[]{:S(2)}) %collective-permute-start.3) | collective-permute-done | bytes 393248 | tf_op jit(solution)/shard_map/ppermute | solution.py:16
  34.9 1.9 %fusion.2 = f32[256]{0:T(256)S(1)} fusion(f32[4096]{0:T(1024)S(1)} %add_rsqrt_fusion, bf16[256,768]{1,0:T(8,128)(2,1)S(1)} %collective-permute-done.3, bf16[4096,768]{1,0:T(8,128)(2,1)S(1)} %copy-done), kind=kOutput, calls=%fused_computation.12 | convolution fusion | flops 1612709632 | bytes 6702080 | tf_op jit(solution)/shard_map/dot_general | solution.py:79
  36.8 7.2 %collective-permute-done.4 = bf16[256,768]{1,0:T(8,128)(2,1)S(1)} collective-permute-done((bf16[256,768]{1,0:T(8,128)(2,1)}, bf16[256,768]{1,0:T(8,128)(2,1)S(1)}, u32[]{:S(2)}, u32[]{:S(2)}) %collective-permute-start.4) | collective-permute-done | bytes 393248 | tf_op jit(solution)/shard_map/ppermute | solution.py:16
  44.0 1.9 %fusion.3 = f32[256]{0:T(256)S(1)} fusion(f32[4096]{0:T(1024)S(1)} %add_rsqrt_fusion, bf16[256,768]{1,0:T(8,128)(2,1)S(1)} %collective-permute-done.4, bf16[4096,768]{1,0:T(8,128)(2,1)S(1)} %copy-done), kind=kOutput, calls=%fused_computation.13 | convolution fusion | flops 1612709632 | bytes 6702080 | tf_op jit(solution)/shard_map/dot_general | solution.py:79
  46.6 3.0 %collective-permute-start.7 = (bf16[256,768]{1,0:T(8,128)(2,1)S(1)}, bf16[256,768]{1,0:T(8,128)(2,1)S(1)}, u32[]{:S(2)}, u32[]{:S(2)}) collective-permute-start(bf16[256,768]{1,0:T(8,128)(2,1)S(1)} %collective-permute-done.4), channel_id=1, source_target_pairs={{0,8},{8,16},{16,24},{24,0},{1,9},{9,17},{17,25},{25,1},{2,10},{10... | collective-permute-start | bytes 1179656 | tf_op jit(solution)/shard_map/ppermute | solution.py:16
  51.1 1.6 %collective-permute-start.10 = (f32[128,896]{1,0:T(8,128)S(1)}, f32[128,896]{1,0:T(8,128)S(1)}, u32[]{:S(2)}, u32[]{:S(2)}) collective-permute-start(f32[128,896]{1,0:T(8,128)S(1)} %slice.83), channel_id=1, source_target_pairs={{0,2},{1,3},{2,0},{3,1},{4,6},{5,7},{6,4},{7,5},{8,10},{9,11},{10,... | collective-permute-start | bytes 1376264 | tf_op jit(solution)/shard_map/ppermute | solution.py:21
  52.6 7.3 %collective-permute-done.6 = bf16[256,768]{1,0:T(8,128)(2,1)S(1)} collective-permute-done((bf16[256,768]{1,0:T(8,128)(2,1)S(1)}, bf16[256,768]{1,0:T(8,128)(2,1)S(1)}, u32[]{:S(2)}, u32[]{:S(2)}) %collective-permute-start.6) | collective-permute-done | bytes 393248 | tf_op jit(solution)/shard_map/ppermute | solution.py:16
  59.9 1.9 %fusion.4 = f32[256]{0:T(256)S(1)} fusion(f32[4096]{0:T(1024)S(1)} %add_rsqrt_fusion, bf16[256,768]{1,0:T(8,128)(2,1)S(1)} %collective-permute-done.6, bf16[4096,768]{1,0:T(8,128)(2,1)S(1)} %copy-done), kind=kOutput, calls=%fused_computation.14 | convolution fusion | flops 1612709632 | bytes 6702080 | tf_op jit(solution)/shard_map/dot_general | solution.py:79
  61.9 1.6 %collective-permute-start.11 = (f32[64,896]{1,0:T(8,128)S(1)}, f32[64,896]{1,0:T(8,128)S(1)}, u32[]{:S(2)}, u32[]{:S(2)}) collective-permute-start(f32[64,896]{1,0:T(8,128)S(1)} %slice.85), channel_id=1, source_target_pairs={{0,4},{1,5},{2,6},{3,7},{4,0},{5,1},{6,2},{7,3},{8,12},{9,13},{10,... | collective-permute-start | bytes 688136 | tf_op jit(solution)/shard_map/ppermute | solution.py:21
  63.5 2.9 %collective-permute-done.7 = bf16[256,768]{1,0:T(8,128)(2,1)S(1)} collective-permute-done((bf16[256,768]{1,0:T(8,128)(2,1)S(1)}, bf16[256,768]{1,0:T(8,128)(2,1)S(1)}, u32[]{:S(2)}, u32[]{:S(2)}) %collective-permute-start.7) | collective-permute-done | bytes 393248 | tf_op jit(solution)/shard_map/ppermute | solution.py:16
  66.4 1.9 %fusion.5 = f32[256]{0:T(256)S(1)} fusion(f32[4096]{0:T(1024)S(1)} %add_rsqrt_fusion, bf16[256,768]{1,0:T(8,128)(2,1)S(1)} %collective-permute-done.7, bf16[4096,768]{1,0:T(8,128)(2,1)S(1)} %copy-done), kind=kOutput, calls=%fused_computation.15 | convolution fusion | flops 1612709632 | bytes 6702080 | tf_op jit(solution)/shard_map/dot_general | solution.py:79
  68.5 1.4 %collective-permute-start.12 = (bf16[16,896]{1,0:T(8,128)(2,1)S(1)}, bf16[16,896]{1,0:T(8,128)(2,1)S(1)}, u32[]{:S(2)}, u32[]{:S(2)}) collective-permute-start(bf16[16,896]{1,0:T(8,128)(2,1)S(1)} %get-tuple-element.9), channel_id=1, source_target_pairs={{0,8},{8,16},{16,24},{24,0},{1,9},{9,17},{17,25},{25,1},{2,10},{10... | collective-permute-start | bytes 86024 | tf_op jit(solution)/shard_map/ppermute | solution.py:16
  69.9 2.5 %collective-permute-start.14 = (bf16[16,896]{1,0:T(8,128)(2,1)S(1)}, bf16[16,896]{1,0:T(8,128)(2,1)S(1)}, u32[]{:S(2)}, u32[]{:S(2)}) collective-permute-start(bf16[16,896]{1,0:T(8,128)(2,1)S(1)} %get-tuple-element.10), channel_id=1, source_target_pairs={{0,24},{8,0},{16,8},{24,16},{1,25},{9,1},{17,9},{25,17},{2,26},{10... | collective-permute-start | bytes 86024 | tf_op jit(solution)/shard_map/ppermute | solution.py:16
  74.5 2.6 %collective-permute-done.13 = bf16[16,896]{1,0:T(8,128)(2,1)S(1)} collective-permute-done((bf16[16,896]{1,0:T(8,128)(2,1)S(1)}, bf16[16,896]{1,0:T(8,128)(2,1)S(1)}, u32[]{:S(2)}, u32[]{:S(2)}) %collective-permute-start.13) | collective-permute-done | bytes 28704 | tf_op jit(solution)/shard_map/ppermute | solution.py:16
  (49 shorter events, 10.1 us)
Async XLA Ops:
  0.6 16.1 %copy-start.1 = (bf16[512,768]{1,0:T(8,128)(2,1)S(1)}, bf16[512,768]{1,0:T(8,128)(2,1)}, u32[]{:S(2)}) copy-start(bf16[512,768]{1,0:T(8,128)(2,1)} %param.6) | copy-start | bytes 2359300
  2.5 18.8 %collective-permute-start = (bf16[256,768]{1,0:T(8,128)(2,1)}, bf16[256,768]{1,0:T(8,128)(2,1)}, u32[]{:S(2)}, u32[]{:S(2)}) collective-permute-start(bf16[256,768]{1,0:T(8,128)(2,1)} %slice.59), channel_id=1, source_target_pairs={{0,8},{8,16},{16,24},{24,0},{1,9},{9,17},{17,25},{25,1},{2,10},{10... | collective-permute-start | bytes 1179656 | tf_op jit(solution)/shard_map/ppermute | solution.py:16
  6.6 19.3 %collective-permute-start.1 = (bf16[256,768]{1,0:T(8,128)(2,1)S(1)}, bf16[256,768]{1,0:T(8,128)(2,1)}, u32[]{:S(2)}, u32[]{:S(2)}) collective-permute-start(bf16[256,768]{1,0:T(8,128)(2,1)S(1)} %slice.77), channel_id=1, source_target_pairs={{0,8},{8,16},{16,24},{24,0},{1,9},{9,17},{17,25},{25,1},{2,10},{10... | collective-permute-start | bytes 1179656 | tf_op jit(solution)/shard_map/ppermute | solution.py:16
  12.4 38.3 %collective-permute-start.9 = (f32[256,896]{1,0:T(8,128)S(1)}, f32[256,896]{1,0:T(8,128)S(1)}, u32[]{:S(2)}, u32[]{:S(2)}) collective-permute-start(f32[256,896]{1,0:T(8,128)S(1)} %fusion.10), channel_id=1, source_target_pairs={{0,1},{1,0},{2,3},{3,2},{4,5},{5,4},{6,7},{7,6},{8,9},{9,8},{10,11... | collective-permute-start | bytes 2752520 | tf_op jit(solution)/shard_map/ppermute | solution.py:21
  12.5 4.6 %copy-start = (bf16[4096,768]{1,0:T(8,128)(2,1)S(1)}, bf16[4096,768]{1,0:T(8,128)(2,1)}, u32[]{:S(2)}) copy-start(bf16[4096,768]{1,0:T(8,128)(2,1)} %param.7) | copy-start | bytes 18874372
  17.1 3.9 %copy-start.2 = (s32[32,4]{0,1:T(4,128)S(1)}, s32[32,4]{0,1:T(4,128)}, u32[]{:S(2)}) copy-start(s32[32,4]{0,1:T(4,128)} %param.8) | copy-start | bytes 1540
  21.3 13.6 %collective-permute-start.3 = (bf16[256,768]{1,0:T(8,128)(2,1)}, bf16[256,768]{1,0:T(8,128)(2,1)S(1)}, u32[]{:S(2)}, u32[]{:S(2)}) collective-permute-start(bf16[256,768]{1,0:T(8,128)(2,1)} %collective-permute-done), channel_id=1, source_target_pairs={{0,8},{8,16},{16,24},{24,0},{1,9},{9,17},{17,25},{25,1},{2,10},{10... | collective-permute-start | bytes 1179656 | tf_op jit(solution)/shard_map/ppermute | solution.py:16
  28.7 20.8 %collective-permute-start.2 = (f32[512]{0:T(512)S(1)}, f32[512]{0:T(512)S(1)}, u32[]{:S(2)}, u32[]{:S(2)}) collective-permute-start(f32[512]{0:T(512)S(1)} %pad_maximum_fusion), channel_id=1, source_target_pairs={{0,24},{8,0},{16,8},{24,16},{1,25},{9,1},{17,9},{25,17},{2,26},{10... | collective-permute-start | bytes 6152 | tf_op jit(solution)/shard_map/ppermute | solution.py:16
  31.1 12.9 %collective-permute-start.4 = (bf16[256,768]{1,0:T(8,128)(2,1)}, bf16[256,768]{1,0:T(8,128)(2,1)S(1)}, u32[]{:S(2)}, u32[]{:S(2)}) collective-permute-start(bf16[256,768]{1,0:T(8,128)(2,1)} %collective-permute-done.1), channel_id=1, source_target_pairs={{0,8},{8,16},{16,24},{24,0},{1,9},{9,17},{17,25},{25,1},{2,10},{10... | collective-permute-start | bytes 1179656 | tf_op jit(solution)/shard_map/ppermute | solution.py:16
  45.9 4.8 %collective-permute-start.5 = (f32[512]{0:T(512)S(1)}, f32[512]{0:T(512)S(1)}, u32[]{:S(2)}, u32[]{:S(2)}) collective-permute-start(f32[512]{0:T(512)S(1)} %pad_maximum_fusion.1), channel_id=1, source_target_pairs={{0,16},{8,24},{16,0},{24,8},{1,17},{9,25},{17,1},{25,9},{2,18},{10... | collective-permute-start | bytes 6152 | tf_op jit(solution)/shard_map/ppermute | solution.py:16
  46.0 13.9 %collective-permute-start.6 = (bf16[256,768]{1,0:T(8,128)(2,1)S(1)}, bf16[256,768]{1,0:T(8,128)(2,1)S(1)}, u32[]{:S(2)}, u32[]{:S(2)}) collective-permute-start(bf16[256,768]{1,0:T(8,128)(2,1)S(1)} %collective-permute-done.3), channel_id=1, source_target_pairs={{0,8},{8,16},{16,24},{24,0},{1,9},{9,17},{17,25},{25,1},{2,10},{10... | collective-permute-start | bytes 1179656 | tf_op jit(solution)/shard_map/ppermute | solution.py:16
  46.6 19.8 %collective-permute-start.7 = (bf16[256,768]{1,0:T(8,128)(2,1)S(1)}, bf16[256,768]{1,0:T(8,128)(2,1)S(1)}, u32[]{:S(2)}, u32[]{:S(2)}) collective-permute-start(bf16[256,768]{1,0:T(8,128)(2,1)S(1)} %collective-permute-done.4), channel_id=1, source_target_pairs={{0,8},{8,16},{16,24},{24,0},{1,9},{9,17},{17,25},{25,1},{2,10},{10... | collective-permute-start | bytes 1179656 | tf_op jit(solution)/shard_map/ppermute | solution.py:16
  51.1 10.8 %collective-permute-start.10 = (f32[128,896]{1,0:T(8,128)S(1)}, f32[128,896]{1,0:T(8,128)S(1)}, u32[]{:S(2)}, u32[]{:S(2)}) collective-permute-start(f32[128,896]{1,0:T(8,128)S(1)} %slice.83), channel_id=1, source_target_pairs={{0,2},{1,3},{2,0},{3,1},{4,6},{5,7},{6,4},{7,5},{8,10},{9,11},{10,... | collective-permute-start | bytes 1376264 | tf_op jit(solution)/shard_map/ppermute | solution.py:21
  61.9 6.5 %collective-permute-start.11 = (f32[64,896]{1,0:T(8,128)S(1)}, f32[64,896]{1,0:T(8,128)S(1)}, u32[]{:S(2)}, u32[]{:S(2)}) collective-permute-start(f32[64,896]{1,0:T(8,128)S(1)} %slice.85), channel_id=1, source_target_pairs={{0,4},{1,5},{2,6},{3,7},{4,0},{5,1},{6,2},{7,3},{8,12},{9,13},{10,... | collective-permute-start | bytes 688136 | tf_op jit(solution)/shard_map/ppermute | solution.py:21
  68.4 5.6 %collective-permute-start.8 = (f32[512]{0:T(512)S(1)}, f32[512]{0:T(512)S(1)}, u32[]{:S(2)}, u32[]{:S(2)}) collective-permute-start(f32[512]{0:T(512)S(1)} %pad_maximum_fusion.2), channel_id=1, source_target_pairs={{0,8},{8,16},{16,24},{24,0},{1,9},{9,17},{17,25},{25,1},{2,10},{10... | collective-permute-start | bytes 6152 | tf_op jit(solution)/shard_map/ppermute | solution.py:16
  68.5 6.0 %collective-permute-start.12 = (bf16[16,896]{1,0:T(8,128)(2,1)S(1)}, bf16[16,896]{1,0:T(8,128)(2,1)S(1)}, u32[]{:S(2)}, u32[]{:S(2)}) collective-permute-start(bf16[16,896]{1,0:T(8,128)(2,1)S(1)} %get-tuple-element.9), channel_id=1, source_target_pairs={{0,8},{8,16},{16,24},{24,0},{1,9},{9,17},{17,25},{25,1},{2,10},{10... | collective-permute-start | bytes 86024 | tf_op jit(solution)/shard_map/ppermute | solution.py:16
  69.9 4.6 %collective-permute-start.14 = (bf16[16,896]{1,0:T(8,128)(2,1)S(1)}, bf16[16,896]{1,0:T(8,128)(2,1)S(1)}, u32[]{:S(2)}, u32[]{:S(2)}) collective-permute-start(bf16[16,896]{1,0:T(8,128)(2,1)S(1)} %get-tuple-element.10), channel_id=1, source_target_pairs={{0,24},{8,0},{16,8},{24,16},{1,25},{9,1},{17,9},{25,17},{2,26},{10... | collective-permute-start | bytes 86024 | tf_op jit(solution)/shard_map/ppermute | solution.py:16
  72.4 4.8 %collective-permute-start.13 = (bf16[16,896]{1,0:T(8,128)(2,1)S(1)}, bf16[16,896]{1,0:T(8,128)(2,1)S(1)}, u32[]{:S(2)}, u32[]{:S(2)}) collective-permute-start(bf16[16,896]{1,0:T(8,128)(2,1)S(1)} %get-tuple-element.11), channel_id=1, source_target_pairs={{0,16},{8,24},{16,0},{24,8},{1,17},{9,25},{17,1},{25,9},{2,18},{10... | collective-permute-start | bytes 86024 | tf_op jit(solution)/shard_map/ppermute | solution.py:16

commit v3 on v2

v3 whole, which is shorter than its diff:
```python
import jax
import jax.numpy as jnp
from jax import lax
from jax.experimental import pallas as pl
from jax.experimental.pallas import tpu as pltpu
from jax.sharding import PartitionSpec as P


CL_DEV = 16
EPS = 1e-06
SPLIT = (1, 1)
PIECES = len(SPLIT)
PREPARE_VMEM = 24 << 20
LANES = 128


def order_of(count):
    return list(range(0, count, 2)) + list(range(count - 1 - count % 2, 0, -2))


def plane_at(place, count):
    return jnp.where(2 * place < count, 2 * place, 2 * (count - 1 - place) + 1)


def place_of(plane, count):
    return jnp.where(plane & 1 == 0, plane >> 1, count - 1 - (plane >> 1))


def shifted(value, axis, steps):
    count = lax.axis_size(axis)
    ring = order_of(count)
    pairs = [(ring[i], ring[(i + steps) % count]) for i in range(count)]
    return lax.ppermute(value, axis, pairs)


def swapped(value, axis, bit):
    count = lax.axis_size(axis)
    return lax.ppermute(value, axis, [(source, source ^ bit) for source in range(count)])


def inverse_norm(values):
    wide = values.astype(jnp.float32)
    return lax.rsqrt(jnp.sum(wide * wide, axis=-1, keepdims=True) + EPS)


def halvings(lanes):
    return lanes.bit_length() - 1


def prepare_body(cycle, lanes, rows_ref, row_ref, owner_ref, local_ref, pattern_ref, *outs):
    keep_ref, send_ref, scale_ref, live_ref = outs
    here = lax.axis_index("blk")
    lane = lax.axis_index("slab")
    rows, width = rows_ref.shape
    entries = row_ref.shape[1]
    levels = halvings(lanes)
    mask = cycle - 1
    spot = place_of(here, cycle)
    wide = rows_ref[...].astype(jnp.float32)
    scale = lax.rsqrt(jnp.sum(wide * wide, axis=-1, keepdims=True) + EPS)
    unit = (wide * scale).astype(jnp.bfloat16)
    scale_ref[...] = jnp.transpose(jnp.broadcast_to(scale, (rows, LANES)))[:1]
    owner = owner_ref[...]
    apart = (owner & (lanes - 1)) ^ lane
    mirrored = jnp.zeros_like(apart)
    for level in range(levels):
        mirrored = mirrored * 2 + ((apart >> level) & 1)
    ahead = (place_of(owner >> levels, cycle) - spot + cycle) & mask
    place = (mirrored * cycle + ahead) * CL_DEV + local_ref[...]
    total = lanes * cycle * CL_DEV
    spread = (lax.broadcasted_iota(jnp.int32, (total, entries), 0) == place).astype(jnp.bfloat16)
    picks = lax.broadcasted_iota(jnp.int32, (rows, entries), 0) == row_ref[...]
    weight = lax.dot_general(
        spread,
        picks.astype(jnp.bfloat16),
        (((1,), (1,)), ((), ())),
        preferred_element_type=jnp.float32,
    ).astype(jnp.bfloat16)
    sums = jnp.dot(weight, unit, preferred_element_type=jnp.float32)
    ones = jnp.ones((entries, LANES), jnp.bfloat16)
    counts = jnp.dot(spread, ones, preferred_element_type=jnp.float32)
    half = total // 2
    keep_ref[:, :width] = sums[:half]
    keep_ref[:, width:] = counts[:half]
    send_ref[:, :width] = sums[half:]
    send_ref[:, width:] = counts[half:]
    pattern = pattern_ref[...]
    column = lax.broadcasted_iota(jnp.int32, pattern.shape, 1) == here * lanes + lane
    mine = jnp.sum(jnp.where(column, pattern, 0), axis=1, keepdims=True)
    span = lax.broadcasted_iota(jnp.int32, mine.shape, 0)
    for step in range(cycle):
        target = plane_at((spot + step) & mask, cycle)
        mark = jnp.sum(jnp.where(span == target, mine, 0), axis=0, keepdims=True)
        live_ref[step : step + 1, :] = jnp.broadcast_to(mark, (1, rows))


def prepare(new_rows, pattern, kept_row, kept_owner, kept_local):
    cycle = lax.axis_size("blk")
    lanes = lax.axis_size("slab")
    assert cycle & (cycle - 1) == 0 and lanes & (lanes - 1) == 0
    rows, width = new_rows.shape
    entries = kept_row.shape[0]
    half = lanes * cycle * CL_DEV // 2
    part = jax.ShapeDtypeStruct((half, width + LANES), jnp.float32)
    return pl.pallas_call(
        lambda *refs: prepare_body(cycle, lanes, *refs),
        out_shape=[
            part,
            part,
            jax.ShapeDtypeStruct((1, rows), jnp.float32),
            jax.ShapeDtypeStruct((cycle, rows), jnp.int32),
        ],
        compiler_params=pltpu.CompilerParams(vmem_limit_bytes=PREPARE_VMEM),
        cost_estimate=pl.CostEstimate(
            flops=4 * half * (entries * rows + rows * width + entries * LANES),
            bytes_accessed=2 * rows * width + 8 * half * (width + LANES),
            transcendentals=rows,
        ),
        name="prepare",
    )(
        new_rows,
        kept_row[None, :],
        kept_owner[:, 0][None, :],
        kept_local[None, :],
        pattern.T,
    )


def kept_sums(keep, send):
    cycle = lax.axis_size("blk")
    lanes = lax.axis_size("slab")
    width = keep.shape[1] - LANES
    for level in range(halvings(lanes)):
        got = swapped(send, "slab", 1 << level)
        whole = keep + got
        half = whole.shape[0] // 2
        keep, send = whole[:half], whole[half:]
    parts = [whole[:CL_DEV]]
    for step in range(1, cycle):
        part = whole[step * CL_DEV : (step + 1) * CL_DEV].astype(jnp.bfloat16)
        parts.append(shifted(part, "blk", step))
    sums = parts[0]
    for part in parts[1:]:
        sums = sums + part.astype(jnp.float32)
    return sums[:, :width], sums[:, width]


def per_device(new_rows, index_rows, pattern, kept_row, kept_owner, kept_local):
    cycle = lax.axis_size("blk")
    rows = new_rows.shape[0]
    index_scale = inverse_norm(index_rows)[:, 0]

    def tile_max(block):
        scores = lax.dot_general(
            block, index_rows, (((1,), (1,)), ((), ())), preferred_element_type=jnp.float32
        )
        return jnp.max(scores * index_scale[None, :], axis=1)

    ends = [rows * sum(SPLIT[: i + 1]) // sum(SPLIT) for i in range(PIECES)]
    moving = [new_rows[: ends[0]]]
    kept_apart = lax.optimization_barrier(new_rows)
    moving += [kept_apart[low:high] for low, high in zip(ends, ends[1:])]
    home = [tile_max(new_rows)]
    for step in range(1, cycle):
        tops = []
        for i in range(PIECES):
            moving[i] = shifted(moving[i], "blk", 1)
            tops.append(tile_max(moving[i]))
        home.append(shifted(jnp.concatenate(tops), "blk", -step))
    keep, send, scale, live = prepare(new_rows, pattern, kept_row, kept_owner, kept_local)
    sums, counts = kept_sums(keep, send)

    def masked(step):
        return jnp.where(live[step] > 0, home[step] * scale[0], jnp.float32(-2.0))

    best = masked(0)
    for step in range(1, cycle - 1):
        best = jnp.maximum(best, masked(step))
    best = lax.optimization_barrier(best)
    best = jnp.maximum(best, masked(cycle - 1))
    return best, sums, counts


def solution(mesh):
    placed = (
        P(("blk", "slab"), None),
        P("blk", None),
        P(),
        P(("blk", "slab")),
        P(("blk", "slab"), None),
        P(("blk", "slab")),
    )
    return jax.shard_map(
        per_device,
        mesh=mesh,
        in_specs=placed,
        out_specs=(P(("blk", "slab")), P(("blk", "slab"), None), P(("blk", "slab"))),
        check_vma=False,
    )
```

time: 78.8 us -> 77.8 us (0.987)
  matrix products: 19.6 us -> 15.4 us
  local copies, waits for them, and re-layouts: 4.58 us -> 7.28 us
  other arithmetic: 7.5 us -> 5.45 us
  waiting for transfers between devices: 26 us -> 27 us
  Pallas kernels: 0 us -> 0.95 us
  starting transfers between devices: 19.8 us -> 20.7 us
    ppermute x3, waiting for transfers between devices: 0.01 us -> 9.46 us  [swapped(): lax.ppermute(value, axis, [(source, source ^ bit) for source in range(cou...]
    ppermute x12, waiting for transfers between devices: 26 us -> 17.5 us  [shifted(): return lax.ppermute(value, axis, pairs)]
    unnamed x6 -> x14, local copies, waits for them, and re-layouts: 0.34 us -> 3.86 us
    dot_general x3 -> x0, matrix products: 2.3 us -> none  [the longest x1 1.67 us: kept_sums(): jnp.dot(pick, new_unit, preferred_element_type=jnp.float32)]
    dot_general x7, matrix products: 17.3 us -> 15.4 us  [tile_max(): lax.dot_general(block, index_rows, (((1,), (1,)), ((), ())), preferred_el...]
    reduce_sum x2 -> x1, other arithmetic: 5.6 us -> 4.53 us  [inverse_norm(): return lax.rsqrt(jnp.sum(wide * wide, axis=-1, keepdims=True) + EPS)]
    pallas_call x0 -> x1, Pallas kernels: none -> 0.95 us  [prepare(): pl.pallas_call(lambda *refs: prepare_body(cycle, lanes, *refs), out_shape...]
    ppermute x12, starting transfers between devices: 16.6 us -> 17.5 us  [shifted(): return lax.ppermute(value, axis, pairs)]
  transfers between devices with their start and end apart: 15 -> 15, of which waited for: 7 -> 7; matrix products, arithmetic and copies ran while one was open for 36% -> 28% of each run, Pallas kernels for 0% -> 1%
where the time goes in v3:
time: 77.8 us; the launch traced here: 77.5 us
  waiting for transfers between devices  27 us (35%)
  starting transfers between devices  20.7 us (27%)
  matrix products  15.4 us (20%)
  local copies, waits for them, and re-layouts  7.28 us (9%)
  other arithmetic  5.45 us (7%)
  Pallas kernels  0.95 us (1%)
  between operations  0.78 us (1%)
    ppermute x12, waiting for transfers between devices, shifted(): return lax.ppermute(value, axis, pairs)  17.5 us
    ppermute x12, starting transfers between devices, shifted(): return lax.ppermute(value, axis, pairs)  17.5 us
    dot_general x7, matrix products, tile_max(): lax.dot_general(block, index_rows, (((1,), (1,)), ((), ())), preferred_el...  15.4 us
    ppermute x3, waiting for transfers between devices, swapped(): lax.ppermute(value, axis, [(source, source ^ bit) for source in range(cou...  9.46 us
    reduce_sum x1, other arithmetic, inverse_norm(): return lax.rsqrt(jnp.sum(wide * wide, axis=-1, keepdims=True) + EPS)  4.53 us
    unnamed x14, local copies, waits for them, and re-layouts  3.86 us
    ppermute x3, starting transfers between devices, swapped(): lax.ppermute(value, axis, [(source, source ^ bit) for source in range(cou...  3.23 us
  transfers between devices with their start and end apart: 15, of which 7 were waited for; matrix products, arithmetic and copies ran while one was open for 28% of the time, Pallas kernels for 1%

profile of v3, /device:TPU:0, one launch (start us, length us, event | category | flops | bytes accessed | tf_op | source)
XLA Modules:
  0.0 77.5 jit_solution(5762154988806598316)
XLA Ops:
  1.7 4.1 %collective-permute-start = (bf16[256,768]{1,0:T(8,128)(2,1)S(1)}, bf16[256,768]{1,0:T(8,128)(2,1)S(1)}, u32[]{:S(2)}, u32[]{:S(2)}) collective-permute-start(bf16[256,768]{1,0:T(8,128)(2,1)S(1)} %slice.53), channel_id=1, source_target_pairs={{0,16},{16,24},{24,8},{8,0},{1,17},{17,25},{25,9},{9,1},{2,18},{18... | collective-permute-start | bytes 1179656 | tf_op jit(solution)/shard_map/ppermute | solution.py:33
  6.9 1.6 %collective-permute-start.1 = (bf16[256,768]{1,0:T(8,128)(2,1)S(1)}, bf16[256,768]{1,0:T(8,128)(2,1)S(1)}, u32[]{:S(2)}, u32[]{:S(2)}) collective-permute-start(bf16[256,768]{1,0:T(8,128)(2,1)S(1)} %slice.67), channel_id=1, source_target_pairs={{0,16},{16,24},{24,8},{8,0},{1,17},{17,25},{25,9},{9,1},{2,18},{18... | collective-permute-start | bytes 1179656 | tf_op jit(solution)/shard_map/ppermute | solution.py:33
  13.4 4.5 %multiply_reduce_fusion = f32[4096]{0:T(1024)S(1)} fusion(bf16[4096,768]{1,0:T(8,128)(2,1)} %param.7), kind=kLoop, calls=%fused_computation | loop fusion | flops 9433088 | bytes 6307840 | tf_op jit(solution)/shard_map/reduce_sum | solution.py:43
  18.0 3.8 %multiply_reduce_fusion.1 = f32[512]{0:T(512)S(1)} fusion(bf16[512,768]{1,0:T(8,128)(2,1)S(1)} %copy-done.1, bf16[4096,768]{1,0:T(8,128)(2,1)S(1)} %copy-done.6, f32[4096]{0:T(1024)S(1)} %add_rsqrt_fusion), kind=kOutput, calls=%fused_computation.1 | convolution fusion | flops 3225419264 | bytes 7096320 | tf_op jit(solution)/shard_map/dot_general | solution.py:154
  22.2 1.9 %fusion = f32[256]{0:T(256)S(1)} fusion(f32[4096]{0:T(1024)S(1)} %add_rsqrt_fusion, bf16[256,768]{1,0:T(8,128)(2,1)S(1)} %collective-permute-done, bf16[4096,768]{1,0:T(8,128)(2,1)S(1)} %copy-done.6), kind=kOutput, calls=%fused_computation.8 | convolution fusion | flops 1612709632 | bytes 6702080 | tf_op jit(solution)/shard_map/dot_general | solution.py:154
  24.1 1.9 %fusion.1 = f32[256]{0:T(256)S(1)} fusion(f32[4096]{0:T(1024)S(1)} %add_rsqrt_fusion, bf16[256,768]{1,0:T(8,128)(2,1)S(1)} %collective-permute-done.1, bf16[4096,768]{1,0:T(8,128)(2,1)S(1)} %copy-done.6), kind=kOutput, calls=%fused_computation.9 | convolution fusion | flops 1612709632 | bytes 6702080 | tf_op jit(solution)/shard_map/dot_general | solution.py:154
  26.1 1.7 %collective-permute-start.2 = (f32[512]{0:T(512)S(1)}, f32[512]{0:T(512)S(1)}, u32[]{:S(2)}, u32[]{:S(2)}) collective-permute-start(f32[512]{0:T(512)S(1)} %pad_maximum_fusion), channel_id=1, source_target_pairs={{0,8},{16,0},{24,16},{8,24},{1,9},{17,1},{25,17},{9,25},{2,10},{18... | collective-permute-start | bytes 6152 | tf_op jit(solution)/shard_map/ppermute | solution.py:33
  27.8 1.2 %collective-permute-start.4 = (bf16[256,768]{1,0:T(8,128)(2,1)S(1)}, bf16[256,768]{1,0:T(8,128)(2,1)S(1)}, u32[]{:S(2)}, u32[]{:S(2)}) collective-permute-start(bf16[256,768]{1,0:T(8,128)(2,1)S(1)} %collective-permute-done.1), channel_id=1, source_target_pairs={{0,16},{16,24},{24,8},{8,0},{1,17},{17,25},{25,9},{9,1},{2,18},{18... | collective-permute-start | bytes 1179656 | tf_op jit(solution)/shard_map/ppermute | solution.py:33
  29.1 4.8 %collective-permute-done.3 = bf16[256,768]{1,0:T(8,128)(2,1)S(1)} collective-permute-done((bf16[256,768]{1,0:T(8,128)(2,1)S(1)}, bf16[256,768]{1,0:T(8,128)(2,1)S(1)}, u32[]{:S(2)}, u32[]{:S(2)}) %collective-permute-start.3) | collective-permute-done | bytes 393248 | tf_op jit(solution)/shard_map/ppermute | solution.py:33
  33.9 1.2 %collective-permute-start.6 = (bf16[256,768]{1,0:T(8,128)(2,1)S(1)}, bf16[256,768]{1,0:T(8,128)(2,1)S(1)}, u32[]{:S(2)}, u32[]{:S(2)}) collective-permute-start(bf16[256,768]{1,0:T(8,128)(2,1)S(1)} %collective-permute-done.3), channel_id=1, source_target_pairs={{0,16},{16,24},{24,8},{8,0},{1,17},{17,25},{25,9},{9,1},{2,18},{18... | collective-permute-start | bytes 1179656 | tf_op jit(solution)/shard_map/ppermute | solution.py:33
  35.1 1.9 %fusion.2 = f32[256]{0:T(256)S(1)} fusion(f32[4096]{0:T(1024)S(1)} %add_rsqrt_fusion, bf16[256,768]{1,0:T(8,128)(2,1)S(1)} %collective-permute-done.3, bf16[4096,768]{1,0:T(8,128)(2,1)S(1)} %copy-done.6), kind=kOutput, calls=%fused_computation.10 | convolution fusion | flops 1612709632 | bytes 6702080 | tf_op jit(solution)/shard_map/dot_general | solution.py:154
  37.0 5.3 %collective-permute-done.4 = bf16[256,768]{1,0:T(8,128)(2,1)S(1)} collective-permute-done((bf16[256,768]{1,0:T(8,128)(2,1)S(1)}, bf16[256,768]{1,0:T(8,128)(2,1)S(1)}, u32[]{:S(2)}, u32[]{:S(2)}) %collective-permute-start.4) | collective-permute-done | bytes 393248 | tf_op jit(solution)/shard_map/ppermute | solution.py:33
  42.3 1.9 %fusion.3 = f32[256]{0:T(256)S(1)} fusion(f32[4096]{0:T(1024)S(1)} %add_rsqrt_fusion, bf16[256,768]{1,0:T(8,128)(2,1)S(1)} %collective-permute-done.4, bf16[4096,768]{1,0:T(8,128)(2,1)S(1)} %copy-done.6), kind=kOutput, calls=%fused_computation.11 | convolution fusion | flops 1612709632 | bytes 6702080 | tf_op jit(solution)/shard_map/dot_general | solution.py:154
  44.3 1.9 %collective-permute-start.5 = (f32[512]{0:T(512)S(1)}, f32[512]{0:T(512)S(1)}, u32[]{:S(2)}, u32[]{:S(2)}) collective-permute-start(f32[512]{0:T(512)S(1)} %pad_maximum_fusion.1), channel_id=1, source_target_pairs={{0,24},{16,8},{24,0},{8,16},{1,25},{17,9},{25,1},{9,17},{2,26},{18... | collective-permute-start | bytes 6152 | tf_op jit(solution)/shard_map/ppermute | solution.py:33
  47.4 4.2 %collective-permute-done.5 = f32[512]{0:T(512)S(1)} collective-permute-done((f32[512]{0:T(512)S(1)}, f32[512]{0:T(512)S(1)}, u32[]{:S(2)}, u32[]{:S(2)}) %collective-permute-start.5) | collective-permute-done | bytes 2080 | tf_op jit(solution)/shard_map/ppermute | solution.py:33
  51.8 1.6 %collective-permute-start.10 = (f32[128,896]{1,0:T(8,128)S(1)}, f32[128,896]{1,0:T(8,128)S(1)}, u32[]{:S(2)}, u32[]{:S(2)}) collective-permute-start(f32[128,896]{1,0:T(8,128)S(1)} %slice.69), channel_id=1, source_target_pairs={{0,2},{1,3},{2,0},{3,1},{4,6},{5,7},{6,4},{7,5},{8,10},{9,11},{10,... | collective-permute-start | bytes 1376264 | tf_op jit(solution)/shard_map/ppermute | solution.py:38
  53.4 1.9 %fusion.4 = f32[256]{0:T(256)S(1)} fusion(f32[4096]{0:T(1024)S(1)} %add_rsqrt_fusion, bf16[256,768]{1,0:T(8,128)(2,1)S(1)} %collective-permute-done.6, bf16[4096,768]{1,0:T(8,128)(2,1)S(1)} %copy-done.6), kind=kOutput, calls=%fused_computation.12 | convolution fusion | flops 1612709632 | bytes 6702080 | tf_op jit(solution)/shard_map/dot_general | solution.py:154
  55.3 7.0 %collective-permute-done.10 = f32[128,896]{1,0:T(8,128)S(1)} collective-permute-done((f32[128,896]{1,0:T(8,128)S(1)}, f32[128,896]{1,0:T(8,128)S(1)}, u32[]{:S(2)}, u32[]{:S(2)}) %collective-permute-start.10) | collective-permute-done | bytes 458784 | tf_op jit(solution)/shard_map/ppermute | solution.py:38
  62.4 1.6 %collective-permute-start.11 = (f32[64,896]{1,0:T(8,128)S(1)}, f32[64,896]{1,0:T(8,128)S(1)}, u32[]{:S(2)}, u32[]{:S(2)}) collective-permute-start(f32[64,896]{1,0:T(8,128)S(1)} %slice.71), channel_id=1, source_target_pairs={{0,4},{1,5},{2,6},{3,7},{4,0},{5,1},{6,2},{7,3},{8,12},{9,13},{10,... | collective-permute-start | bytes 688136 | tf_op jit(solution)/shard_map/ppermute | solution.py:38
  64.0 1.9 %fusion.5 = f32[256]{0:T(256)S(1)} fusion(f32[4096]{0:T(1024)S(1)} %add_rsqrt_fusion, bf16[256,768]{1,0:T(8,128)(2,1)S(1)} %collective-permute-done.7, bf16[4096,768]{1,0:T(8,128)(2,1)S(1)} %copy-done.6), kind=kOutput, calls=%fused_computation.13 | convolution fusion | flops 1612709632 | bytes 6702080 | tf_op jit(solution)/shard_map/dot_general | solution.py:154
  66.0 2.5 %collective-permute-done.11 = f32[64,896]{1,0:T(8,128)S(1)} collective-permute-done((f32[64,896]{1,0:T(8,128)S(1)}, f32[64,896]{1,0:T(8,128)S(1)}, u32[]{:S(2)}, u32[]{:S(2)}) %collective-permute-start.11) | collective-permute-done | bytes 229408 | tf_op jit(solution)/shard_map/ppermute | solution.py:38
  68.6 2.0 %collective-permute-start.14 = (bf16[16,896]{1,0:T(8,128)(2,1)S(1)}, bf16[16,896]{1,0:T(8,128)(2,1)S(1)}, u32[]{:S(2)}, u32[]{:S(2)}) collective-permute-start(bf16[16,896]{1,0:T(8,128)(2,1)S(1)} %get-tuple-element.18), channel_id=1, source_target_pairs={{0,8},{16,0},{24,16},{8,24},{1,9},{17,1},{25,17},{9,25},{2,10},{18... | collective-permute-start | bytes 86024 | tf_op jit(solution)/shard_map/ppermute | solution.py:33
  70.6 1.9 %collective-permute-start.13 = (bf16[16,896]{1,0:T(8,128)(2,1)S(1)}, bf16[16,896]{1,0:T(8,128)(2,1)S(1)}, u32[]{:S(2)}, u32[]{:S(2)}) collective-permute-start(bf16[16,896]{1,0:T(8,128)(2,1)S(1)} %get-tuple-element.19), channel_id=1, source_target_pairs={{0,24},{16,8},{24,0},{8,16},{1,25},{17,9},{25,1},{9,17},{2,26},{18... | collective-permute-start | bytes 86024 | tf_op jit(solution)/shard_map/ppermute | solution.py:33
  73.4 2.9 %collective-permute-done.13 = bf16[16,896]{1,0:T(8,128)(2,1)S(1)} collective-permute-done((bf16[16,896]{1,0:T(8,128)(2,1)S(1)}, bf16[16,896]{1,0:T(8,128)(2,1)S(1)}, u32[]{:S(2)}, u32[]{:S(2)}) %collective-permute-start.13) | collective-permute-done | bytes 28704 | tf_op jit(solution)/shard_map/ppermute | solution.py:33
  (47 shorter events, 11.3 us)
Async XLA Ops:
  0.6 17.3 %copy-start.1 = (bf16[512,768]{1,0:T(8,128)(2,1)S(1)}, bf16[512,768]{1,0:T(8,128)(2,1)}, u32[]{:S(2)}) copy-start(bf16[512,768]{1,0:T(8,128)(2,1)} %refs_0_.1) | copy-start | bytes 2359300
  1.7 20.1 %collective-permute-start = (bf16[256,768]{1,0:T(8,128)(2,1)S(1)}, bf16[256,768]{1,0:T(8,128)(2,1)S(1)}, u32[]{:S(2)}, u32[]{:S(2)}) collective-permute-start(bf16[256,768]{1,0:T(8,128)(2,1)S(1)} %slice.53), channel_id=1, source_target_pairs={{0,16},{16,24},{24,8},{8,0},{1,17},{17,25},{25,9},{9,1},{2,18},{18... | collective-permute-start | bytes 1179656 | tf_op jit(solution)/shard_map/ppermute | solution.py:33
  6.9 17.3 %collective-permute-start.1 = (bf16[256,768]{1,0:T(8,128)(2,1)S(1)}, bf16[256,768]{1,0:T(8,128)(2,1)S(1)}, u32[]{:S(2)}, u32[]{:S(2)}) collective-permute-start(bf16[256,768]{1,0:T(8,128)(2,1)S(1)} %slice.67), channel_id=1, source_target_pairs={{0,16},{16,24},{24,8},{8,0},{1,17},{17,25},{25,9},{9,1},{2,18},{18... | collective-permute-start | bytes 1179656 | tf_op jit(solution)/shard_map/ppermute | solution.py:33
  8.5 1.1 %copy-start = (bf16[512,768]{1,0:T(8,128)(2,1)S(1)}, bf16[512,768]{1,0:T(8,128)(2,1)}, u32[]{:S(2)}) copy-start(bf16[512,768]{1,0:T(8,128)(2,1)} %refs_0_.1) | copy-start | bytes 2359300
  9.6 0.7 copy-start.2
  10.3 0.7 copy-start.3
  11.0 0.7 copy-start.4
  11.7 0.7 copy-start.5
  12.4 5.6 %copy-start.6 = (bf16[4096,768]{1,0:T(8,128)(2,1)S(1)}, bf16[4096,768]{1,0:T(8,128)(2,1)}, u32[]{:S(2)}) copy-start(bf16[4096,768]{1,0:T(8,128)(2,1)} %param.7) | copy-start | bytes 18874372
  13.3 38.3 %collective-permute-start.9 = (f32[256,896]{1,0:T(8,128)S(1)}, f32[256,896]{1,0:T(8,128)S(1)}, u32[]{:S(2)}, u32[]{:S(2)}) collective-permute-start(f32[256,896]{1,0:T(8,128)S(1)} %get-tuple-element.10), channel_id=1, source_target_pairs={{0,1},{1,0},{2,3},{3,2},{4,5},{5,4},{6,7},{7,6},{8,9},{9,8},{10,11... | collective-permute-start | bytes 2752520 | tf_op jit(solution)/shard_map/ppermute | solution.py:38
  21.8 12.1 %collective-permute-start.3 = (bf16[256,768]{1,0:T(8,128)(2,1)S(1)}, bf16[256,768]{1,0:T(8,128)(2,1)S(1)}, u32[]{:S(2)}, u32[]{:S(2)}) collective-permute-start(bf16[256,768]{1,0:T(8,128)(2,1)S(1)} %collective-permute-done), channel_id=1, source_target_pairs={{0,16},{16,24},{24,8},{8,0},{1,17},{17,25},{25,9},{9,1},{2,18},{18... | collective-permute-start | bytes 1179656 | tf_op jit(solution)/shard_map/ppermute | solution.py:33
  26.1 21.3 %collective-permute-start.2 = (f32[512]{0:T(512)S(1)}, f32[512]{0:T(512)S(1)}, u32[]{:S(2)}, u32[]{:S(2)}) collective-permute-start(f32[512]{0:T(512)S(1)} %pad_maximum_fusion), channel_id=1, source_target_pairs={{0,8},{16,0},{24,16},{8,24},{1,9},{17,1},{25,17},{9,25},{2,10},{18... | collective-permute-start | bytes 6152 | tf_op jit(solution)/shard_map/ppermute | solution.py:33
  27.8 14.5 %collective-permute-start.4 = (bf16[256,768]{1,0:T(8,128)(2,1)S(1)}, bf16[256,768]{1,0:T(8,128)(2,1)S(1)}, u32[]{:S(2)}, u32[]{:S(2)}) collective-permute-start(bf16[256,768]{1,0:T(8,128)(2,1)S(1)} %collective-permute-done.1), channel_id=1, source_target_pairs={{0,16},{16,24},{24,8},{8,0},{1,17},{17,25},{25,9},{9,1},{2,18},{18... | collective-permute-start | bytes 1179656 | tf_op jit(solution)/shard_map/ppermute | solution.py:33
  33.9 19.5 %collective-permute-start.6 = (bf16[256,768]{1,0:T(8,128)(2,1)S(1)}, bf16[256,768]{1,0:T(8,128)(2,1)S(1)}, u32[]{:S(2)}, u32[]{:S(2)}) collective-permute-start(bf16[256,768]{1,0:T(8,128)(2,1)S(1)} %collective-permute-done.3), channel_id=1, source_target_pairs={{0,16},{16,24},{24,8},{8,0},{1,17},{17,25},{25,9},{9,1},{2,18},{18... | collective-permute-start | bytes 1179656 | tf_op jit(solution)/shard_map/ppermute | solution.py:33
  44.3 7.4 %collective-permute-start.5 = (f32[512]{0:T(512)S(1)}, f32[512]{0:T(512)S(1)}, u32[]{:S(2)}, u32[]{:S(2)}) collective-permute-start(f32[512]{0:T(512)S(1)} %pad_maximum_fusion.1), channel_id=1, source_target_pairs={{0,24},{16,8},{24,0},{8,16},{1,25},{17,9},{25,1},{9,17},{2,26},{18... | collective-permute-start | bytes 6152 | tf_op jit(solution)/shard_map/ppermute | solution.py:33
  46.2 17.8 %collective-permute-start.7 = (bf16[256,768]{1,0:T(8,128)(2,1)S(1)}, bf16[256,768]{1,0:T(8,128)(2,1)S(1)}, u32[]{:S(2)}, u32[]{:S(2)}) collective-permute-start(bf16[256,768]{1,0:T(8,128)(2,1)S(1)} %collective-permute-done.4), channel_id=1, source_target_pairs={{0,16},{16,24},{24,8},{8,0},{1,17},{17,25},{25,9},{9,1},{2,18},{18... | collective-permute-start | bytes 1179656 | tf_op jit(solution)/shard_map/ppermute | solution.py:33
  51.8 10.5 %collective-permute-start.10 = (f32[128,896]{1,0:T(8,128)S(1)}, f32[128,896]{1,0:T(8,128)S(1)}, u32[]{:S(2)}, u32[]{:S(2)}) collective-permute-start(f32[128,896]{1,0:T(8,128)S(1)} %slice.69), channel_id=1, source_target_pairs={{0,2},{1,3},{2,0},{3,1},{4,6},{5,7},{6,4},{7,5},{8,10},{9,11},{10,... | collective-permute-start | bytes 1376264 | tf_op jit(solution)/shard_map/ppermute | solution.py:38
  62.4 6.1 %collective-permute-start.11 = (f32[64,896]{1,0:T(8,128)S(1)}, f32[64,896]{1,0:T(8,128)S(1)}, u32[]{:S(2)}, u32[]{:S(2)}) collective-permute-start(f32[64,896]{1,0:T(8,128)S(1)} %slice.71), channel_id=1, source_target_pairs={{0,4},{1,5},{2,6},{3,7},{4,0},{5,1},{6,2},{7,3},{8,12},{9,13},{10,... | collective-permute-start | bytes 688136 | tf_op jit(solution)/shard_map/ppermute | solution.py:38
  65.9 6.6 %collective-permute-start.8 = (f32[512]{0:T(512)S(1)}, f32[512]{0:T(512)S(1)}, u32[]{:S(2)}, u32[]{:S(2)}) collective-permute-start(f32[512]{0:T(512)S(1)} %pad_maximum_fusion.2), channel_id=1, source_target_pairs={{0,16},{16,24},{24,8},{8,0},{1,17},{17,25},{25,9},{9,1},{2,18},{18... | collective-permute-start | bytes 6152 | tf_op jit(solution)/shard_map/ppermute | solution.py:33
  68.5 4.6 %collective-permute-start.12 = (bf16[16,896]{1,0:T(8,128)(2,1)S(1)}, bf16[16,896]{1,0:T(8,128)(2,1)S(1)}, u32[]{:S(2)}, u32[]{:S(2)}) collective-permute-start(bf16[16,896]{1,0:T(8,128)(2,1)S(1)} %get-tuple-element.17), channel_id=1, source_target_pairs={{0,16},{16,24},{24,8},{8,0},{1,17},{17,25},{25,9},{9,1},{2,18},{18... | collective-permute-start | bytes 86024 | tf_op jit(solution)/shard_map/ppermute | solution.py:33
  68.6 4.8 %collective-permute-start.14 = (bf16[16,896]{1,0:T(8,128)(2,1)S(1)}, bf16[16,896]{1,0:T(8,128)(2,1)S(1)}, u32[]{:S(2)}, u32[]{:S(2)}) collective-permute-start(bf16[16,896]{1,0:T(8,128)(2,1)S(1)} %get-tuple-element.18), channel_id=1, source_target_pairs={{0,8},{16,0},{24,16},{8,24},{1,9},{17,1},{25,17},{9,25},{2,10},{18... | collective-permute-start | bytes 86024 | tf_op jit(solution)/shard_map/ppermute | solution.py:33
  70.6 5.7 %collective-permute-start.13 = (bf16[16,896]{1,0:T(8,128)(2,1)S(1)}, bf16[16,896]{1,0:T(8,128)(2,1)S(1)}, u32[]{:S(2)}, u32[]{:S(2)}) collective-permute-start(bf16[16,896]{1,0:T(8,128)(2,1)S(1)} %get-tuple-element.19), channel_id=1, source_target_pairs={{0,24},{16,8},{24,0},{8,16},{1,25},{17,9},{25,1},{9,17},{2,26},{18... | collective-permute-start | bytes 86024 | tf_op jit(solution)/shard_map/ppermute | solution.py:33

commit v4 on v3

--- a/solution.py
+++ b/solution.py
@@ -129,7 +129,6 @@
 def kept_sums(keep, send):
     cycle = lax.axis_size("blk")
     lanes = lax.axis_size("slab")
-    width = keep.shape[1] - LANES
     for level in range(halvings(lanes)):
         got = swapped(send, "slab", 1 << level)
         whole = keep + got
@@ -137,12 +136,45 @@
         keep, send = whole[:half], whole[half:]
     parts = [whole[:CL_DEV]]
     for step in range(1, cycle):
-        part = whole[step * CL_DEV : (step + 1) * CL_DEV].astype(jnp.bfloat16)
+        part = whole[step * CL_DEV : (step + 1) * CL_DEV]
         parts.append(shifted(part, "blk", step))
-    sums = parts[0]
+    return parts
+
+
+def finish_body(cycle, *refs):
+    parts, tops = refs[:cycle], refs[cycle : 2 * cycle - 1]
+    scale_ref, live_ref, sums_ref, counts_ref, early_ref = refs[2 * cycle - 1 :]
+    width = sums_ref.shape[1]
+    total = parts[0][...]
     for part in parts[1:]:
-        sums = sums + part.astype(jnp.float32)
-    return sums[:, :width], sums[:, width]
+        total = total + part[...].astype(jnp.float32)
+    sums_ref[...] = total[:, :width]
+    counts_ref[...] = jnp.transpose(total[:, width:])[:1]
+    best = jnp.full(early_ref.shape, -2.0, jnp.float32)
+    for step, top in enumerate(tops):
+        value = jnp.where(live_ref[step : step + 1, :] > 0, top[...] * scale_ref[...], -2.0)
+        best = jnp.maximum(best, value)
+    early_ref[...] = best
+
+
+def finish(parts, tops, scale, live):
+    cycle = len(parts)
+    width = parts[0].shape[1] - LANES
+    return pl.pallas_call(
+        lambda *refs: finish_body(cycle, *refs),
+        out_shape=[
+            jax.ShapeDtypeStruct((CL_DEV, width), jnp.float32),
+            jax.ShapeDtypeStruct((1, CL_DEV), jnp.float32),
+            jax.ShapeDtypeStruct(scale.shape, jnp.float32),
+        ],
+        compiler_params=pltpu.CompilerParams(vmem_limit_bytes=8 << 20),
+        cost_estimate=pl.CostEstimate(
+            flops=2 * cycle * CL_DEV * width,
+            bytes_accessed=4 * cycle * CL_DEV * width,
+            transcendentals=0,
+        ),
+        name="finish",
+    )(*parts, *[top[None, :] for top in tops], scale, live)
 
 
 def per_device(new_rows, index_rows, pattern, kept_row, kept_owner, kept_local):
@@ -168,17 +200,10 @@
             tops.append(tile_max(moving[i]))
         home.append(shifted(jnp.concatenate(tops), "blk", -step))
     keep, send, scale, live = prepare(new_rows, pattern, kept_row, kept_owner, kept_local)
-    sums, counts = kept_sums(keep, send)
-
-    def masked(step):
-        return jnp.where(live[step] > 0, home[step] * scale[0], jnp.float32(-2.0))
-
-    best = masked(0)
-    for step in range(1, cycle - 1):
-        best = jnp.maximum(best, masked(step))
-    best = lax.optimization_barrier(best)
-    best = jnp.maximum(best, masked(cycle - 1))
-    return best, sums, counts
+    parts = kept_sums(keep, send)
+    sums, counts, early = finish(parts, home[:-1], scale, live)
+    last = jnp.where(live[cycle - 1] > 0, home[-1] * scale[0], jnp.float32(-2.0))
+    return jnp.maximum(early[0], last), sums, counts[0]
 
 
 def solution(mesh):

time: 77.8 us -> 78.5 us (level)
  starting transfers between devices: 20.7 us -> 28.2 us
  waiting for transfers between devices: 27 us -> 23.5 us
  local copies, waits for them, and re-layouts: 7.28 us -> 3.97 us
    ppermute x12, starting transfers between devices: 17.5 us -> 24.5 us  [shifted(): return lax.ppermute(value, axis, pairs)]
    ppermute x12, waiting for transfers between devices: 17.5 us -> 15.2 us  [shifted(): return lax.ppermute(value, axis, pairs)]
    slice x3 -> x1, local copies, waits for them, and re-layouts: 1.26 us -> 0.02 us  [kept_sums(): part = whole[step * CL_DEV:(step + 1) * CL_DEV]]
    ppermute x3, waiting for transfers between devices: 9.46 us -> 8.24 us  [swapped(): lax.ppermute(value, axis, [(source, source ^ bit) for source in range(cou...]
    slice x1, local copies, waits for them, and re-layouts: 1.09 us -> 0.03 us  [per_device(): moving = [new_rows[:ends[0]]]]
    slice x1, local copies, waits for them, and re-layouts: 1.02 us -> 0.03 us  [per_device(): moving += [kept_apart[low:high] for low, high in zip(ends, ends[1:])]]
  transfers between devices with their start and end apart: 15 -> 15, of which waited for: 7 -> 9; matrix products, arithmetic and copies ran while one was open for 28% -> 25% of each run, Pallas kernels for 1% -> 1%
where the time goes in v4:
time: 78.5 us; the launch traced here: 78.2 us
  starting transfers between devices  28.2 us (36%)
  waiting for transfers between devices  23.5 us (30%)
  matrix products  15.3 us (19%)
  other arithmetic  4.92 us (6%)
  local copies, waits for them, and re-layouts  3.97 us (5%)
  Pallas kernels  1.59 us (2%)
    ppermute x12, starting transfers between devices, shifted(): return lax.ppermute(value, axis, pairs)  24.5 us
    dot_general x7, matrix products, tile_max(): lax.dot_general(block, index_rows, (((1,), (1,)), ((), ())), preferred_el...  15.3 us
    ppermute x12, waiting for transfers between devices, shifted(): return lax.ppermute(value, axis, pairs)  15.2 us
    ppermute x3, waiting for transfers between devices, swapped(): lax.ppermute(value, axis, [(source, source ^ bit) for source in range(cou...  8.24 us
    reduce_sum x1, other arithmetic, inverse_norm(): return lax.rsqrt(jnp.sum(wide * wide, axis=-1, keepdims=True) + EPS)  4.08 us
    unnamed x14, local copies, waits for them, and re-layouts  3.85 us
    ppermute x3, starting transfers between devices, swapped(): lax.ppermute(value, axis, [(source, source ^ bit) for source in range(cou...  3.7 us
  transfers between devices with their start and end apart: 15, of which 9 were waited for; matrix products, arithmetic and copies ran while one was open for 25% of the time, Pallas kernels for 1%

profile of v4, /device:TPU:0, one launch (start us, length us, event | category | flops | bytes accessed | tf_op | source)
XLA Modules:
  0.0 78.2 jit_solution(13748013052650526191)
XLA Ops:
  6.0 3.6 %collective-permute-start.6 = (bf16[256,768]{1,0:T(8,128)(2,1)S(1)}, bf16[256,768]{1,0:T(8,128)(2,1)S(1)}, u32[]{:S(2)}, u32[]{:S(2)}) collective-permute-start(bf16[256,768]{1,0:T(8,128)(2,1)S(1)} %slice.41), channel_id=1, source_target_pairs={{0,16},{16,24},{24,8},{8,0},{1,17},{17,25},{25,9},{9,1},{2,18},{18... | collective-permute-start | bytes 1179656 | tf_op jit(solution)/shard_map/ppermute | solution.py:33
  9.7 1.6 %collective-permute-start.7 = (bf16[256,768]{1,0:T(8,128)(2,1)S(1)}, bf16[256,768]{1,0:T(8,128)(2,1)S(1)}, u32[]{:S(2)}, u32[]{:S(2)}) collective-permute-start(bf16[256,768]{1,0:T(8,128)(2,1)S(1)} %slice.52), channel_id=1, source_target_pairs={{0,16},{16,24},{24,8},{8,0},{1,17},{17,25},{25,9},{9,1},{2,18},{18... | collective-permute-start | bytes 1179656 | tf_op jit(solution)/shard_map/ppermute | solution.py:33
  11.3 4.1 %multiply_reduce_fusion = f32[4096]{0:T(1024)S(1)} fusion(bf16[4096,768]{1,0:T(8,128)(2,1)} %param.7), kind=kLoop, calls=%fused_computation | loop fusion | flops 9433088 | bytes 6307840 | tf_op jit(solution)/shard_map/reduce_sum | solution.py:43
  15.5 3.8 %multiply_reduce_fusion.1 = f32[512]{0:T(512)S(1)} fusion(bf16[512,768]{1,0:T(8,128)(2,1)S(1)} %copy-done.1, bf16[4096,768]{1,0:T(8,128)(2,1)S(1)} %copy-done.6, f32[4096]{0:T(1024)S(1)} %add_rsqrt_fusion), kind=kOutput, calls=%fused_computation.1 | convolution fusion | flops 3225419264 | bytes 7096320 | tf_op jit(solution)/shard_map/dot_general | solution.py:186
  19.3 3.3 %collective-permute-start.9 = (bf16[256,768]{1,0:T(8,128)(2,1)S(1)}, bf16[256,768]{1,0:T(8,128)(2,1)S(1)}, u32[]{:S(2)}, u32[]{:S(2)}) collective-permute-start(bf16[256,768]{1,0:T(8,128)(2,1)S(1)} %collective-permute-done.6), channel_id=1, source_target_pairs={{0,16},{16,24},{24,8},{8,0},{1,17},{17,25},{25,9},{9,1},{2,18},{18... | collective-permute-start | bytes 1179656 | tf_op jit(solution)/shard_map/ppermute | solution.py:33
  22.6 1.9 %fusion = f32[256]{0:T(256)S(1)} fusion(f32[4096]{0:T(1024)S(1)} %add_rsqrt_fusion, bf16[256,768]{1,0:T(8,128)(2,1)S(1)} %collective-permute-done.6, bf16[4096,768]{1,0:T(8,128)(2,1)S(1)} %copy-done.6), kind=kOutput, calls=%fused_computation.8 | convolution fusion | flops 1612709632 | bytes 6702080 | tf_op jit(solution)/shard_map/dot_general | solution.py:186
  24.5 3.1 %collective-permute-done.7 = bf16[256,768]{1,0:T(8,128)(2,1)S(1)} collective-permute-done((bf16[256,768]{1,0:T(8,128)(2,1)S(1)}, bf16[256,768]{1,0:T(8,128)(2,1)S(1)}, u32[]{:S(2)}, u32[]{:S(2)}) %collective-permute-start.7) | collective-permute-done | bytes 393248 | tf_op jit(solution)/shard_map/ppermute | solution.py:33
  27.6 1.9 %fusion.1 = f32[256]{0:T(256)S(1)} fusion(f32[4096]{0:T(1024)S(1)} %add_rsqrt_fusion, bf16[256,768]{1,0:T(8,128)(2,1)S(1)} %collective-permute-done.7, bf16[4096,768]{1,0:T(8,128)(2,1)S(1)} %copy-done.6), kind=kOutput, calls=%fused_computation.9 | convolution fusion | flops 1612709632 | bytes 6702080 | tf_op jit(solution)/shard_map/dot_general | solution.py:186
  29.5 2.4 %collective-permute-start.8 = (f32[512]{0:T(512)S(1)}, f32[512]{0:T(512)S(1)}, u32[]{:S(2)}, u32[]{:S(2)}) collective-permute-start(f32[512]{0:T(512)S(1)} %pad_maximum_fusion), channel_id=1, source_target_pairs={{0,8},{16,0},{24,16},{8,24},{1,9},{17,1},{25,17},{9,25},{2,10},{18... | collective-permute-start | bytes 6152 | tf_op jit(solution)/shard_map/ppermute | solution.py:33
  33.0 3.0 %collective-permute-done.9 = bf16[256,768]{1,0:T(8,128)(2,1)S(1)} collective-permute-done((bf16[256,768]{1,0:T(8,128)(2,1)S(1)}, bf16[256,768]{1,0:T(8,128)(2,1)S(1)}, u32[]{:S(2)}, u32[]{:S(2)}) %collective-permute-start.9) | collective-permute-done | bytes 393248 | tf_op jit(solution)/shard_map/ppermute | solution.py:33
  36.0 1.9 %fusion.2 = f32[256]{0:T(256)S(1)} fusion(f32[4096]{0:T(1024)S(1)} %add_rsqrt_fusion, bf16[256,768]{1,0:T(8,128)(2,1)S(1)} %collective-permute-done.9, bf16[4096,768]{1,0:T(8,128)(2,1)S(1)} %copy-done.6), kind=kOutput, calls=%fused_computation.10 | convolution fusion | flops 1612709632 | bytes 6702080 | tf_op jit(solution)/shard_map/dot_general | solution.py:186
  37.9 3.5 %collective-permute-start.12 = (bf16[256,768]{1,0:T(8,128)(2,1)S(1)}, bf16[256,768]{1,0:T(8,128)(2,1)S(1)}, u32[]{:S(2)}, u32[]{:S(2)}) collective-permute-start(bf16[256,768]{1,0:T(8,128)(2,1)S(1)} %collective-permute-done.9), channel_id=1, source_target_pairs={{0,16},{16,24},{24,8},{8,0},{1,17},{17,25},{25,9},{9,1},{2,18},{18... | collective-permute-start | bytes 1179656 | tf_op jit(solution)/shard_map/ppermute | solution.py:33
  41.4 3.1 %collective-permute-done.10 = bf16[256,768]{1,0:T(8,128)(2,1)S(1)} collective-permute-done((bf16[256,768]{1,0:T(8,128)(2,1)S(1)}, bf16[256,768]{1,0:T(8,128)(2,1)S(1)}, u32[]{:S(2)}, u32[]{:S(2)}) %collective-permute-start.10) | collective-permute-done | bytes 393248 | tf_op jit(solution)/shard_map/ppermute | solution.py:33
  44.5 1.9 %fusion.3 = f32[256]{0:T(256)S(1)} fusion(f32[4096]{0:T(1024)S(1)} %add_rsqrt_fusion, bf16[256,768]{1,0:T(8,128)(2,1)S(1)} %collective-permute-done.10, bf16[4096,768]{1,0:T(8,128)(2,1)S(1)} %copy-done.6), kind=kOutput, calls=%fused_computation.11 | convolution fusion | flops 1612709632 | bytes 6702080 | tf_op jit(solution)/shard_map/dot_general | solution.py:186
  46.4 3.6 %collective-permute-start.11 = (f32[512]{0:T(512)S(1)}, f32[512]{0:T(512)S(1)}, u32[]{:S(2)}, u32[]{:S(2)}) collective-permute-start(f32[512]{0:T(512)S(1)} %pad_maximum_fusion.1), channel_id=1, source_target_pairs={{0,24},{16,8},{24,0},{8,16},{1,25},{17,9},{25,1},{9,17},{2,26},{18... | collective-permute-start | bytes 6152 | tf_op jit(solution)/shard_map/ppermute | solution.py:33
  50.5 1.6 %collective-permute-start.1 = (f32[128,896]{1,0:T(8,128)S(1)}, f32[128,896]{1,0:T(8,128)S(1)}, u32[]{:S(2)}, u32[]{:S(2)}) collective-permute-start(f32[128,896]{1,0:T(8,128)S(1)} %slice.45), channel_id=1, source_target_pairs={{0,2},{1,3},{2,0},{3,1},{4,6},{5,7},{6,4},{7,5},{8,10},{9,11},{10,... | collective-permute-start | bytes 1376264 | tf_op jit(solution)/shard_map/ppermute | solution.py:38
  52.9 1.9 %fusion.4 = f32[256]{0:T(256)S(1)} fusion(f32[4096]{0:T(1024)S(1)} %add_rsqrt_fusion, bf16[256,768]{1,0:T(8,128)(2,1)S(1)} %collective-permute-done.12, bf16[4096,768]{1,0:T(8,128)(2,1)S(1)} %copy-done.6), kind=kOutput, calls=%fused_computation.12 | convolution fusion | flops 1612709632 | bytes 6702080 | tf_op jit(solution)/shard_map/dot_general | solution.py:186
  54.9 6.8 %collective-permute-done.1 = f32[128,896]{1,0:T(8,128)S(1)} collective-permute-done((f32[128,896]{1,0:T(8,128)S(1)}, f32[128,896]{1,0:T(8,128)S(1)}, u32[]{:S(2)}, u32[]{:S(2)}) %collective-permute-start.1) | collective-permute-done | bytes 458784 | tf_op jit(solution)/shard_map/ppermute | solution.py:38
  61.7 1.6 %collective-permute-start.2 = (f32[64,896]{1,0:T(8,128)S(1)}, f32[64,896]{1,0:T(8,128)S(1)}, u32[]{:S(2)}, u32[]{:S(2)}) collective-permute-start(f32[64,896]{1,0:T(8,128)S(1)} %slice.47), channel_id=1, source_target_pairs={{0,4},{1,5},{2,6},{3,7},{4,0},{5,1},{6,2},{7,3},{8,12},{9,13},{10,... | collective-permute-start | bytes 688136 | tf_op jit(solution)/shard_map/ppermute | solution.py:38
  63.3 1.9 %fusion.5 = f32[256]{0:T(256)S(1)} fusion(f32[4096]{0:T(1024)S(1)} %add_rsqrt_fusion, bf16[256,768]{1,0:T(8,128)(2,1)S(1)} %collective-permute-done.13, bf16[4096,768]{1,0:T(8,128)(2,1)S(1)} %copy-done.6), kind=kOutput, calls=%fused_computation.13 | convolution fusion | flops 1612709632 | bytes 6702080 | tf_op jit(solution)/shard_map/dot_general | solution.py:186
  66.3 1.5 %collective-permute-done.2 = f32[64,896]{1,0:T(8,128)S(1)} collective-permute-done((f32[64,896]{1,0:T(8,128)S(1)}, f32[64,896]{1,0:T(8,128)S(1)}, u32[]{:S(2)}, u32[]{:S(2)}) %collective-permute-start.2) | collective-permute-done | bytes 229408 | tf_op jit(solution)/shard_map/ppermute | solution.py:38
  68.6 3.3 %collective-permute-start.4 = (f32[16,896]{1,0:T(8,128)S(1)}, f32[16,896]{1,0:T(8,128)S(1)}, u32[]{:S(2)}, u32[]{:S(2)}) collective-permute-start(f32[16,896]{1,0:T(8,128)S(1)} %get-tuple-element.18), channel_id=1, source_target_pairs={{0,24},{16,8},{24,0},{8,16},{1,25},{17,9},{25,1},{9,17},{2,26},{18... | collective-permute-start | bytes 172040 | tf_op jit(solution)/shard_map/ppermute | solution.py:33
  72.6 2.1 %collective-permute-done.4.refs_2_ = f32[16,896]{1,0:T(8,128)S(1)} collective-permute-done((f32[16,896]{1,0:T(8,128)S(1)}, f32[16,896]{1,0:T(8,128)S(1)}, u32[]{:S(2)}, u32[]{:S(2)}) %collective-permute-start.4) | collective-permute-done | bytes 57376 | tf_op jit(solution)/shard_map/ppermute | solution.py:33
  74.8 2.2 %collective-permute-done.5.refs_3_ = f32[16,896]{1,0:T(8,128)S(1)} collective-permute-done((f32[16,896]{1,0:T(8,128)S(1)}, f32[16,896]{1,0:T(8,128)S(1)}, u32[]{:S(2)}, u32[]{:S(2)}) %collective-permute-start.5) | collective-permute-done | bytes 57376 | tf_op jit(solution)/shard_map/ppermute | solution.py:33
  (44 shorter events, 11.8 us)
Async XLA Ops:
  0.6 1.1 %copy-start = (bf16[512,768]{1,0:T(8,128)(2,1)S(1)}, bf16[512,768]{1,0:T(8,128)(2,1)}, u32[]{:S(2)}) copy-start(bf16[512,768]{1,0:T(8,128)(2,1)} %refs_0_.1) | copy-start | bytes 2359300
  1.8 0.7 copy-start.2
  2.4 0.7 copy-start.3
  3.1 0.7 copy-start.4
  3.8 0.7 copy-start.5
  4.5 11.0 %copy-start.1 = (bf16[512,768]{1,0:T(8,128)(2,1)S(1)}, bf16[512,768]{1,0:T(8,128)(2,1)}, u32[]{:S(2)}) copy-start(bf16[512,768]{1,0:T(8,128)(2,1)} %refs_0_.1) | copy-start | bytes 2359300
  4.5 11.0 %copy-start.6 = (bf16[4096,768]{1,0:T(8,128)(2,1)S(1)}, bf16[4096,768]{1,0:T(8,128)(2,1)}, u32[]{:S(2)}) copy-start(bf16[4096,768]{1,0:T(8,128)(2,1)} %param.7) | copy-start | bytes 18874372
  5.4 44.9 %collective-permute-start = (f32[256,896]{1,0:T(8,128)S(1)}, f32[256,896]{1,0:T(8,128)S(1)}, u32[]{:S(2)}, u32[]{:S(2)}) collective-permute-start(f32[256,896]{1,0:T(8,128)S(1)} %get-tuple-element.11), channel_id=1, source_target_pairs={{0,1},{1,0},{2,3},{3,2},{4,5},{5,4},{6,7},{7,6},{8,9},{9,8},{10,11... | collective-permute-start | bytes 2752520 | tf_op jit(solution)/shard_map/ppermute | solution.py:38
  6.0 13.3 %collective-permute-start.6 = (bf16[256,768]{1,0:T(8,128)(2,1)S(1)}, bf16[256,768]{1,0:T(8,128)(2,1)S(1)}, u32[]{:S(2)}, u32[]{:S(2)}) collective-permute-start(bf16[256,768]{1,0:T(8,128)(2,1)S(1)} %slice.41), channel_id=1, source_target_pairs={{0,16},{16,24},{24,8},{8,0},{1,17},{17,25},{25,9},{9,1},{2,18},{18... | collective-permute-start | bytes 1179656 | tf_op jit(solution)/shard_map/ppermute | solution.py:33
  9.7 17.9 %collective-permute-start.7 = (bf16[256,768]{1,0:T(8,128)(2,1)S(1)}, bf16[256,768]{1,0:T(8,128)(2,1)S(1)}, u32[]{:S(2)}, u32[]{:S(2)}) collective-permute-start(bf16[256,768]{1,0:T(8,128)(2,1)S(1)} %slice.52), channel_id=1, source_target_pairs={{0,16},{16,24},{24,8},{8,0},{1,17},{17,25},{25,9},{9,1},{2,18},{18... | collective-permute-start | bytes 1179656 | tf_op jit(solution)/shard_map/ppermute | solution.py:33
  19.3 16.7 %collective-permute-start.9 = (bf16[256,768]{1,0:T(8,128)(2,1)S(1)}, bf16[256,768]{1,0:T(8,128)(2,1)S(1)}, u32[]{:S(2)}, u32[]{:S(2)}) collective-permute-start(bf16[256,768]{1,0:T(8,128)(2,1)S(1)} %collective-permute-done.6), channel_id=1, source_target_pairs={{0,16},{16,24},{24,8},{8,0},{1,17},{17,25},{25,9},{9,1},{2,18},{18... | collective-permute-start | bytes 1179656 | tf_op jit(solution)/shard_map/ppermute | solution.py:33
  29.5 42.4 %collective-permute-start.8 = (f32[512]{0:T(512)S(1)}, f32[512]{0:T(512)S(1)}, u32[]{:S(2)}, u32[]{:S(2)}) collective-permute-start(f32[512]{0:T(512)S(1)} %pad_maximum_fusion), channel_id=1, source_target_pairs={{0,8},{16,0},{24,16},{8,24},{1,9},{17,1},{25,17},{9,25},{2,10},{18... | collective-permute-start | bytes 6152 | tf_op jit(solution)/shard_map/ppermute | solution.py:33
  31.9 12.6 %collective-permute-start.10 = (bf16[256,768]{1,0:T(8,128)(2,1)S(1)}, bf16[256,768]{1,0:T(8,128)(2,1)S(1)}, u32[]{:S(2)}, u32[]{:S(2)}) collective-permute-start(bf16[256,768]{1,0:T(8,128)(2,1)S(1)} %collective-permute-done.7), channel_id=1, source_target_pairs={{0,16},{16,24},{24,8},{8,0},{1,17},{17,25},{25,9},{9,1},{2,18},{18... | collective-permute-start | bytes 1179656 | tf_op jit(solution)/shard_map/ppermute | solution.py:33
  37.9 15.0 %collective-permute-start.12 = (bf16[256,768]{1,0:T(8,128)(2,1)S(1)}, bf16[256,768]{1,0:T(8,128)(2,1)S(1)}, u32[]{:S(2)}, u32[]{:S(2)}) collective-permute-start(bf16[256,768]{1,0:T(8,128)(2,1)S(1)} %collective-permute-done.9), channel_id=1, source_target_pairs={{0,16},{16,24},{24,8},{8,0},{1,17},{17,25},{25,9},{9,1},{2,18},{18... | collective-permute-start | bytes 1179656 | tf_op jit(solution)/shard_map/ppermute | solution.py:33
  46.4 25.5 %collective-permute-start.11 = (f32[512]{0:T(512)S(1)}, f32[512]{0:T(512)S(1)}, u32[]{:S(2)}, u32[]{:S(2)}) collective-permute-start(f32[512]{0:T(512)S(1)} %pad_maximum_fusion.1), channel_id=1, source_target_pairs={{0,24},{16,8},{24,0},{8,16},{1,25},{17,9},{25,1},{9,17},{2,26},{18... | collective-permute-start | bytes 6152 | tf_op jit(solution)/shard_map/ppermute | solution.py:33
  50.0 13.3 %collective-permute-start.13 = (bf16[256,768]{1,0:T(8,128)(2,1)S(1)}, bf16[256,768]{1,0:T(8,128)(2,1)S(1)}, u32[]{:S(2)}, u32[]{:S(2)}) collective-permute-start(bf16[256,768]{1,0:T(8,128)(2,1)S(1)} %collective-permute-done.10), channel_id=1, source_target_pairs={{0,16},{16,24},{24,8},{8,0},{1,17},{17,25},{25,9},{9,1},{2,18},{18... | collective-permute-start | bytes 1179656 | tf_op jit(solution)/shard_map/ppermute | solution.py:33
  50.5 11.2 %collective-permute-start.1 = (f32[128,896]{1,0:T(8,128)S(1)}, f32[128,896]{1,0:T(8,128)S(1)}, u32[]{:S(2)}, u32[]{:S(2)}) collective-permute-start(f32[128,896]{1,0:T(8,128)S(1)} %slice.45), channel_id=1, source_target_pairs={{0,2},{1,3},{2,0},{3,1},{4,6},{5,7},{6,4},{7,5},{8,10},{9,11},{10,... | collective-permute-start | bytes 1376264 | tf_op jit(solution)/shard_map/ppermute | solution.py:38
  61.7 6.1 %collective-permute-start.2 = (f32[64,896]{1,0:T(8,128)S(1)}, f32[64,896]{1,0:T(8,128)S(1)}, u32[]{:S(2)}, u32[]{:S(2)}) collective-permute-start(f32[64,896]{1,0:T(8,128)S(1)} %slice.47), channel_id=1, source_target_pairs={{0,4},{1,5},{2,6},{3,7},{4,0},{5,1},{6,2},{7,3},{8,12},{9,13},{10,... | collective-permute-start | bytes 688136 | tf_op jit(solution)/shard_map/ppermute | solution.py:38
  65.2 12.4 %collective-permute-start.14 = (f32[512]{0:T(512)S(1)}, f32[512]{0:T(512)S(1)}, u32[]{:S(2)}, u32[]{:S(2)}) collective-permute-start(f32[512]{0:T(512)S(1)} %pad_maximum_fusion.2), channel_id=1, source_target_pairs={{0,16},{16,24},{24,8},{8,0},{1,17},{17,25},{25,9},{9,1},{2,18},{18... | collective-permute-start | bytes 6152 | tf_op jit(solution)/shard_map/ppermute | solution.py:33
  67.9 4.8 %collective-permute-start.3 = (f32[16,896]{1,0:T(8,128)S(1)}, f32[16,896]{1,0:T(8,128)S(1)}, u32[]{:S(2)}, u32[]{:S(2)}) collective-permute-start(f32[16,896]{1,0:T(8,128)S(1)} %get-tuple-element.19), channel_id=1, source_target_pairs={{0,16},{16,24},{24,8},{8,0},{1,17},{17,25},{25,9},{9,1},{2,18},{18... | collective-permute-start | bytes 172040 | tf_op jit(solution)/shard_map/ppermute | solution.py:33
  68.6 6.2 %collective-permute-start.4 = (f32[16,896]{1,0:T(8,128)S(1)}, f32[16,896]{1,0:T(8,128)S(1)}, u32[]{:S(2)}, u32[]{:S(2)}) collective-permute-start(f32[16,896]{1,0:T(8,128)S(1)} %get-tuple-element.18), channel_id=1, source_target_pairs={{0,24},{16,8},{24,0},{8,16},{1,25},{17,9},{25,1},{9,17},{2,26},{18... | collective-permute-start | bytes 172040 | tf_op jit(solution)/shard_map/ppermute | solution.py:33
  71.9 5.1 %collective-permute-start.5 = (f32[16,896]{1,0:T(8,128)S(1)}, f32[16,896]{1,0:T(8,128)S(1)}, u32[]{:S(2)}, u32[]{:S(2)}) collective-permute-start(f32[16,896]{1,0:T(8,128)S(1)} %get-tuple-element.17), channel_id=1, source_target_pairs={{0,8},{16,0},{24,16},{8,24},{1,9},{17,1},{25,17},{9,25},{2,10},{18... | collective-permute-start | bytes 172040 | tf_op jit(solution)/shard_map/ppermute | solution.py:33

commit v5 on v4

--- a/solution.py
+++ b/solution.py
@@ -8,8 +8,7 @@
 
 CL_DEV = 16
 EPS = 1e-06
-SPLIT = (1, 1)
-PIECES = len(SPLIT)
+PIECES = 2
 PREPARE_VMEM = 24 << 20
 LANES = 128
 
@@ -136,7 +135,7 @@
         keep, send = whole[:half], whole[half:]
     parts = [whole[:CL_DEV]]
     for step in range(1, cycle):
-        part = whole[step * CL_DEV : (step + 1) * CL_DEV]
+        part = whole[step * CL_DEV : (step + 1) * CL_DEV].astype(jnp.bfloat16)
         parts.append(shifted(part, "blk", step))
     return parts
 
@@ -188,16 +187,23 @@
         )
         return jnp.max(scores * index_scale[None, :], axis=1)
 
-    ends = [rows * sum(SPLIT[: i + 1]) // sum(SPLIT) for i in range(PIECES)]
-    moving = [new_rows[: ends[0]]]
-    kept_apart = lax.optimization_barrier(new_rows)
-    moving += [kept_apart[low:high] for low, high in zip(ends, ends[1:])]
+    half = rows // PIECES
     home = [tile_max(new_rows)]
-    for step in range(1, cycle):
+    arrived = shifted(new_rows, "blk", 1)
+    top = tile_max(arrived)
+    home.append(shifted(top, "blk", -1))
+    second = shifted(lax.optimization_barrier(new_rows)[half:], "blk", -1)
+    second_top = tile_max(second)
+    moving = [arrived[:half], arrived[half:]]
+    for step in range(2, cycle):
+        if step == cycle - 1:
+            moving.pop()
         tops = []
-        for i in range(PIECES):
+        for i in range(len(moving)):
             moving[i] = shifted(moving[i], "blk", 1)
             tops.append(tile_max(moving[i]))
+        if step == cycle - 1:
+            tops.append(second_top)
         home.append(shifted(jnp.concatenate(tops), "blk", -step))
     keep, send, scale, live = prepare(new_rows, pattern, kept_row, kept_owner, kept_local)
     parts = kept_sums(keep, send)

time: 78.5 us -> 74.7 us (0.952)
  starting transfers between devices: 28.2 us -> 19.5 us
  waiting for transfers between devices: 23.5 us -> 27.9 us
    ppermute x12 -> x11, waiting for transfers between devices: 15.2 us -> 27.9 us  [shifted(): return lax.ppermute(value, axis, pairs)]
    ppermute x3, waiting for transfers between devices: 8.24 us -> 0.01 us  [swapped(): lax.ppermute(value, axis, [(source, source ^ bit) for source in range(cou...]
    ppermute x12 -> x11, starting transfers between devices: 24.5 us -> 16.3 us  [shifted(): return lax.ppermute(value, axis, pairs)]
    dot_general x7 -> x6, matrix products: 15.3 us -> 15.3 us  [tile_max(): lax.dot_general(block, index_rows, (((1,), (1,)), ((), ())), preferred_el...]
  transfers between devices with their start and end apart: 15 -> 14, of which waited for: 9 -> 7; matrix products, arithmetic and copies ran while one was open for 25% -> 27% of each run, Pallas kernels for 1% -> 2%
where the time goes in v5:
time: 74.7 us; the launch traced here: 74.5 us
  waiting for transfers between devices  27.9 us (37%)
  starting transfers between devices  19.5 us (26%)
  matrix products  15.3 us (20%)
  other arithmetic  5.39 us (7%)
  local copies, waits for them, and re-layouts  4.03 us (5%)
  Pallas kernels  1.59 us (2%)
  between operations  0.79 us (1%)
    ppermute x11, waiting for transfers between devices, shifted(): return lax.ppermute(value, axis, pairs)  27.9 us
    ppermute x11, starting transfers between devices, shifted(): return lax.ppermute(value, axis, pairs)  16.3 us
    dot_general x6, matrix products, tile_max(): lax.dot_general(block, index_rows, (((1,), (1,)), ((), ())), preferred_el...  15.3 us
    reduce_sum x1, other arithmetic, inverse_norm(): return lax.rsqrt(jnp.sum(wide * wide, axis=-1, keepdims=True) + EPS)  4.56 us
    unnamed x14, local copies, waits for them, and re-layouts  3.89 us
    ppermute x3, starting transfers between devices, swapped(): lax.ppermute(value, axis, [(source, source ^ bit) for source in range(cou...  3.22 us
  transfers between devices with their start and end apart: 14, of which 7 were waited for; matrix products, arithmetic and copies ran while one was open for 27% of the time, Pallas kernels for 2%

profile of v5, /device:TPU:0, one launch (start us, length us, event | category | flops | bytes accessed | tf_op | source)
XLA Modules:
  0.0 74.5 jit_solution(8102141975161334597)
XLA Ops:
  0.6 4.1 %collective-permute-start.6 = (bf16[512,768]{1,0:T(8,128)(2,1)}, bf16[512,768]{1,0:T(8,128)(2,1)S(1)}, u32[]{:S(2)}, u32[]{:S(2)}) collective-permute-start(bf16[512,768]{1,0:T(8,128)(2,1)} %refs_0_.1), channel_id=1, source_target_pairs={{0,16},{16,24},{24,8},{8,0},{1,17},{17,25},{25,9},{9,1},{2,18},{18... | collective-permute-start | bytes 2359304 | tf_op jit(solution)/shard_map/ppermute | solution.py:32
  4.8 1.2 %copy-done = bf16[512,768]{1,0:T(8,128)(2,1)S(1)} copy-done((bf16[512,768]{1,0:T(8,128)(2,1)S(1)}, bf16[512,768]{1,0:T(8,128)(2,1)}, u32[]{:S(2)}) %copy-start) | copy-done | bytes 786456
  5.9 0.7 copy-done.2
  8.6 1.0 %prepare.1 = (f32[256,896]{1,0:T(8,128)S(1)}, f32[256,896]{1,0:T(8,128)S(1)}, f32[1,512]{1,0:T(1,128)S(1)}, s32[4,512]{1,0:T(4,128)S(1)}) custom-call(bf16[512,768]{1,0:T(8,128)(2,1)S(1)} %copy-done, s32[1,256]{1,0:T(1,128)S(1)} %bitcast.28, s32[1,256]{1,0:T(1,128)S(1)} %bitcast.29, s32[1,256]{1,0:T(1,128)S(1)} %bitcast.30, s32[4,32]{1,0:T(4,128)S(1)} %bitcast.27), custom_call_target="tpu_custom_call" | custom-call | flops 570425344 | bytes 2621440 | tf_op jit(solution)/shard_map/prepare/pallas_call | solution.py:104
  9.8 4.6 %multiply_reduce_fusion = f32[4096]{0:T(1024)S(1)} fusion(bf16[4096,768]{1,0:T(8,128)(2,1)} %param.7), kind=kLoop, calls=%fused_computation | loop fusion | flops 9433088 | bytes 6307840 | tf_op jit(solution)/shard_map/reduce_sum | solution.py:42
  14.4 3.8 %multiply_reduce_fusion.2 = f32[512]{0:T(512)S(1)} fusion(bf16[512,768]{1,0:T(8,128)(2,1)S(1)} %copy-done.1, bf16[4096,768]{1,0:T(8,128)(2,1)S(1)} %copy-done.6, f32[4096]{0:T(1024)S(1)} %add_rsqrt_fusion), kind=kOutput, calls=%fused_computation.2 | convolution fusion | flops 3225419264 | bytes 7096320 | tf_op jit(solution)/shard_map/dot_general | solution.py:185
  18.2 13.8 %collective-permute-done.12 = bf16[256,768]{1,0:T(8,128)(2,1)S(1)} collective-permute-done((bf16[256,768]{1,0:T(8,128)(2,1)S(1)}, bf16[256,768]{1,0:T(8,128)(2,1)S(1)}, u32[]{:S(2)}, u32[]{:S(2)}) %collective-permute-start.12) | collective-permute-done | bytes 393248 | tf_op jit(solution)/shard_map/ppermute | solution.py:32
  32.0 1.9 %fusion.3 = f32[256]{0:T(256)S(1)} fusion(f32[4096]{0:T(1024)S(1)} %add_rsqrt_fusion, bf16[256,768]{1,0:T(8,128)(2,1)S(1)} %collective-permute-done.12, bf16[4096,768]{1,0:T(8,128)(2,1)S(1)} %copy-done.6), kind=kOutput, calls=%fused_computation.10 | convolution fusion | flops 1612709632 | bytes 6702080 | tf_op jit(solution)/shard_map/dot_general | solution.py:185
  34.6 2.4 %collective-permute-start.9 = (bf16[256,768]{1,0:T(8,128)(2,1)S(1)}, bf16[256,768]{1,0:T(8,128)(2,1)S(1)}, u32[]{:S(2)}, u32[]{:S(2)}) collective-permute-start(bf16[256,768]{1,0:T(8,128)(2,1)S(1)} %get-tuple-element.20), channel_id=1, source_target_pairs={{0,16},{16,24},{24,8},{8,0},{1,17},{17,25},{25,9},{9,1},{2,18},{18... | collective-permute-start | bytes 1179656 | tf_op jit(solution)/shard_map/ppermute | solution.py:32
  37.1 3.8 %multiply_reduce_fusion.1 = f32[512]{0:T(512)S(1)} fusion(bf16[512,768]{1,0:T(8,128)(2,1)S(1)} %collective-permute-done.6, bf16[4096,768]{1,0:T(8,128)(2,1)S(1)} %copy-done.6, f32[4096]{0:T(1024)S(1)} %add_rsqrt_fusion), kind=kOutput, calls=%fused_computation.1 | convolution fusion | flops 3225419264 | bytes 7096320 | tf_op jit(solution)/shard_map/dot_general | solution.py:185
  41.1 1.6 %collective-permute-start.1 = (f32[128,896]{1,0:T(8,128)S(1)}, f32[128,896]{1,0:T(8,128)S(1)}, u32[]{:S(2)}, u32[]{:S(2)}) collective-permute-start(f32[128,896]{1,0:T(8,128)S(1)} %slice.52), channel_id=1, source_target_pairs={{0,2},{1,3},{2,0},{3,1},{4,6},{5,7},{6,4},{7,5},{8,10},{9,11},{10,... | collective-permute-start | bytes 1376264 | tf_op jit(solution)/shard_map/ppermute | solution.py:37
  42.7 3.4 %collective-permute-done.8 = bf16[256,768]{1,0:T(8,128)(2,1)S(1)} collective-permute-done((bf16[256,768]{1,0:T(8,128)(2,1)S(1)}, bf16[256,768]{1,0:T(8,128)(2,1)S(1)}, u32[]{:S(2)}, u32[]{:S(2)}) %collective-permute-start.8) | collective-permute-done | bytes 393248 | tf_op jit(solution)/shard_map/ppermute | solution.py:32
  46.0 1.5 %collective-permute-start.11 = (bf16[256,768]{1,0:T(8,128)(2,1)S(1)}, bf16[256,768]{1,0:T(8,128)(2,1)S(1)}, u32[]{:S(2)}, u32[]{:S(2)}) collective-permute-start(bf16[256,768]{1,0:T(8,128)(2,1)S(1)} %collective-permute-done.8), channel_id=1, source_target_pairs={{0,16},{16,24},{24,8},{8,0},{1,17},{17,25},{25,9},{9,1},{2,18},{18... | collective-permute-start | bytes 1179656 | tf_op jit(solution)/shard_map/ppermute | solution.py:32
  47.6 1.9 %fusion = f32[256]{0:T(256)S(1)} fusion(f32[4096]{0:T(1024)S(1)} %add_rsqrt_fusion, bf16[256,768]{1,0:T(8,128)(2,1)S(1)} %collective-permute-done.8, bf16[4096,768]{1,0:T(8,128)(2,1)S(1)} %copy-done.6), kind=kOutput, calls=%fused_computation.7 | convolution fusion | flops 1612709632 | bytes 6702080 | tf_op jit(solution)/shard_map/dot_general | solution.py:185
  49.5 5.0 %collective-permute-done.9 = bf16[256,768]{1,0:T(8,128)(2,1)S(1)} collective-permute-done((bf16[256,768]{1,0:T(8,128)(2,1)S(1)}, bf16[256,768]{1,0:T(8,128)(2,1)S(1)}, u32[]{:S(2)}, u32[]{:S(2)}) %collective-permute-start.9) | collective-permute-done | bytes 393248 | tf_op jit(solution)/shard_map/ppermute | solution.py:32
  54.5 1.9 %fusion.1 = f32[256]{0:T(256)S(1)} fusion(f32[4096]{0:T(1024)S(1)} %add_rsqrt_fusion, bf16[256,768]{1,0:T(8,128)(2,1)S(1)} %collective-permute-done.9, bf16[4096,768]{1,0:T(8,128)(2,1)S(1)} %copy-done.6), kind=kOutput, calls=%fused_computation.8 | convolution fusion | flops 1612709632 | bytes 6702080 | tf_op jit(solution)/shard_map/dot_general | solution.py:185
  56.4 2.5 %collective-permute-start.10 = (f32[512]{0:T(512)S(1)}, f32[512]{0:T(512)S(1)}, u32[]{:S(2)}, u32[]{:S(2)}) collective-permute-start(f32[512]{0:T(512)S(1)} %pad_maximum_fusion), channel_id=1, source_target_pairs={{0,24},{16,8},{24,0},{8,16},{1,25},{17,9},{25,1},{9,17},{2,26},{18... | collective-permute-start | bytes 6152 | tf_op jit(solution)/shard_map/ppermute | solution.py:32
  59.0 1.6 %collective-permute-start.2 = (f32[64,896]{1,0:T(8,128)S(1)}, f32[64,896]{1,0:T(8,128)S(1)}, u32[]{:S(2)}, u32[]{:S(2)}) collective-permute-start(f32[64,896]{1,0:T(8,128)S(1)} %slice.54), channel_id=1, source_target_pairs={{0,4},{1,5},{2,6},{3,7},{4,0},{5,1},{6,2},{7,3},{8,12},{9,13},{10,... | collective-permute-start | bytes 688136 | tf_op jit(solution)/shard_map/ppermute | solution.py:37
  60.6 1.4 %collective-permute-done.11 = bf16[256,768]{1,0:T(8,128)(2,1)S(1)} collective-permute-done((bf16[256,768]{1,0:T(8,128)(2,1)S(1)}, bf16[256,768]{1,0:T(8,128)(2,1)S(1)}, u32[]{:S(2)}, u32[]{:S(2)}) %collective-permute-start.11) | collective-permute-done | bytes 393248 | tf_op jit(solution)/shard_map/ppermute | solution.py:32
  62.0 1.9 %fusion.2 = f32[256]{0:T(256)S(1)} fusion(f32[4096]{0:T(1024)S(1)} %add_rsqrt_fusion, bf16[256,768]{1,0:T(8,128)(2,1)S(1)} %collective-permute-done.11, bf16[4096,768]{1,0:T(8,128)(2,1)S(1)} %copy-done.6), kind=kOutput, calls=%fused_computation.9 | convolution fusion | flops 1612709632 | bytes 6702080 | tf_op jit(solution)/shard_map/dot_general | solution.py:185
  64.0 1.3 %collective-permute-start.13 = (f32[512]{0:T(512)S(1)}, f32[512]{0:T(512)S(1)}, u32[]{:S(2)}, u32[]{:S(2)}) collective-permute-start(f32[512]{0:T(512)S(1)} %pad_maximum_fusion.1), channel_id=1, source_target_pairs={{0,16},{16,24},{24,8},{8,0},{1,17},{17,25},{25,9},{9,1},{2,18},{18... | collective-permute-start | bytes 6152 | tf_op jit(solution)/shard_map/ppermute | solution.py:32
  65.3 1.9 %collective-permute-start.3 = (bf16[16,896]{1,0:T(8,128)(2,1)S(1)}, bf16[16,896]{1,0:T(8,128)(2,1)S(1)}, u32[]{:S(2)}, u32[]{:S(2)}) collective-permute-start(bf16[16,896]{1,0:T(8,128)(2,1)S(1)} %get-tuple-element.23), channel_id=1, source_target_pairs={{0,16},{16,24},{24,8},{8,0},{1,17},{17,25},{25,9},{9,1},{2,18},{18... | collective-permute-start | bytes 86024 | tf_op jit(solution)/shard_map/ppermute | solution.py:32
  67.2 1.3 %collective-permute-start.4 = (bf16[16,896]{1,0:T(8,128)(2,1)S(1)}, bf16[16,896]{1,0:T(8,128)(2,1)S(1)}, u32[]{:S(2)}, u32[]{:S(2)}) collective-permute-start(bf16[16,896]{1,0:T(8,128)(2,1)S(1)} %get-tuple-element.22), channel_id=1, source_target_pairs={{0,24},{16,8},{24,0},{8,16},{1,25},{17,9},{25,1},{9,17},{2,26},{18... | collective-permute-start | bytes 86024 | tf_op jit(solution)/shard_map/ppermute | solution.py:32
  69.2 3.6 %collective-permute-done.4.refs_2_ = bf16[16,896]{1,0:T(8,128)(2,1)S(1)} collective-permute-done((bf16[16,896]{1,0:T(8,128)(2,1)S(1)}, bf16[16,896]{1,0:T(8,128)(2,1)S(1)}, u32[]{:S(2)}, u32[]{:S(2)}) %collective-permute-start.4) | collective-permute-done | bytes 28704 | tf_op jit(solution)/shard_map/ppermute | solution.py:32
  (41 shorter events, 5.6 us)
Async XLA Ops:
  0.6 33.3 %collective-permute-start.6 = (bf16[512,768]{1,0:T(8,128)(2,1)}, bf16[512,768]{1,0:T(8,128)(2,1)S(1)}, u32[]{:S(2)}, u32[]{:S(2)}) collective-permute-start(bf16[512,768]{1,0:T(8,128)(2,1)} %refs_0_.1), channel_id=1, source_target_pairs={{0,16},{16,24},{24,8},{8,0},{1,17},{17,25},{25,9},{9,1},{2,18},{18... | collective-permute-start | bytes 2359304 | tf_op jit(solution)/shard_map/ppermute | solution.py:32
  4.7 1.2 %copy-start = (bf16[512,768]{1,0:T(8,128)(2,1)S(1)}, bf16[512,768]{1,0:T(8,128)(2,1)}, u32[]{:S(2)}) copy-start(bf16[512,768]{1,0:T(8,128)(2,1)} %refs_0_.1) | copy-start | bytes 2359300
  5.9 0.7 copy-start.2
  6.6 0.7 copy-start.3
  7.3 0.7 copy-start.4
  8.0 0.7 copy-start.5
  8.6 5.7 %copy-start.1 = (bf16[512,768]{1,0:T(8,128)(2,1)S(1)}, bf16[512,768]{1,0:T(8,128)(2,1)}, u32[]{:S(2)}) copy-start(bf16[512,768]{1,0:T(8,128)(2,1)} %refs_0_.1) | copy-start | bytes 2359300
  8.6 5.7 %copy-start.6 = (bf16[4096,768]{1,0:T(8,128)(2,1)S(1)}, bf16[4096,768]{1,0:T(8,128)(2,1)}, u32[]{:S(2)}) copy-start(bf16[4096,768]{1,0:T(8,128)(2,1)} %param.7) | copy-start | bytes 18874372
  9.6 31.4 %collective-permute-start = (f32[256,896]{1,0:T(8,128)S(1)}, f32[256,896]{1,0:T(8,128)S(1)}, u32[]{:S(2)}, u32[]{:S(2)}) collective-permute-start(f32[256,896]{1,0:T(8,128)S(1)} %get-tuple-element.11), channel_id=1, source_target_pairs={{0,1},{1,0},{2,3},{3,2},{4,5},{5,4},{6,7},{7,6},{8,9},{9,8},{10,11... | collective-permute-start | bytes 2752520 | tf_op jit(solution)/shard_map/ppermute | solution.py:37
  9.7 22.3 %collective-permute-start.12 = (bf16[256,768]{1,0:T(8,128)(2,1)S(1)}, bf16[256,768]{1,0:T(8,128)(2,1)S(1)}, u32[]{:S(2)}, u32[]{:S(2)}) collective-permute-start(bf16[256,768]{1,0:T(8,128)(2,1)S(1)} %slice.61), channel_id=1, source_target_pairs={{0,8},{16,0},{24,16},{8,24},{1,9},{17,1},{25,17},{9,25},{2,10},{18... | collective-permute-start | bytes 1179656 | tf_op jit(solution)/shard_map/ppermute | solution.py:32
  34.0 12.1 %collective-permute-start.8 = (bf16[256,768]{1,0:T(8,128)(2,1)S(1)}, bf16[256,768]{1,0:T(8,128)(2,1)S(1)}, u32[]{:S(2)}, u32[]{:S(2)}) collective-permute-start(bf16[256,768]{1,0:T(8,128)(2,1)S(1)} %get-tuple-element.19), channel_id=1, source_target_pairs={{0,16},{16,24},{24,8},{8,0},{1,17},{17,25},{25,9},{9,1},{2,18},{18... | collective-permute-start | bytes 1179656 | tf_op jit(solution)/shard_map/ppermute | solution.py:32
  34.6 19.8 %collective-permute-start.9 = (bf16[256,768]{1,0:T(8,128)(2,1)S(1)}, bf16[256,768]{1,0:T(8,128)(2,1)S(1)}, u32[]{:S(2)}, u32[]{:S(2)}) collective-permute-start(bf16[256,768]{1,0:T(8,128)(2,1)S(1)} %get-tuple-element.20), channel_id=1, source_target_pairs={{0,16},{16,24},{24,8},{8,0},{1,17},{17,25},{25,9},{9,1},{2,18},{18... | collective-permute-start | bytes 1179656 | tf_op jit(solution)/shard_map/ppermute | solution.py:32
  40.9 27.6 %collective-permute-start.7 = (f32[512]{0:T(512)S(1)}, f32[512]{0:T(512)S(1)}, u32[]{:S(2)}, u32[]{:S(2)}) collective-permute-start(f32[512]{0:T(512)S(1)} %multiply_reduce_fusion.1), channel_id=1, source_target_pairs={{0,8},{16,0},{24,16},{8,24},{1,9},{17,1},{25,17},{9,25},{2,10},{18... | collective-permute-start | bytes 6152 | tf_op jit(solution)/shard_map/ppermute | solution.py:32
  41.1 17.8 %collective-permute-start.1 = (f32[128,896]{1,0:T(8,128)S(1)}, f32[128,896]{1,0:T(8,128)S(1)}, u32[]{:S(2)}, u32[]{:S(2)}) collective-permute-start(f32[128,896]{1,0:T(8,128)S(1)} %slice.52), channel_id=1, source_target_pairs={{0,2},{1,3},{2,0},{3,1},{4,6},{5,7},{6,4},{7,5},{8,10},{9,11},{10,... | collective-permute-start | bytes 1376264 | tf_op jit(solution)/shard_map/ppermute | solution.py:37
  46.0 16.0 %collective-permute-start.11 = (bf16[256,768]{1,0:T(8,128)(2,1)S(1)}, bf16[256,768]{1,0:T(8,128)(2,1)S(1)}, u32[]{:S(2)}, u32[]{:S(2)}) collective-permute-start(bf16[256,768]{1,0:T(8,128)(2,1)S(1)} %collective-permute-done.8), channel_id=1, source_target_pairs={{0,16},{16,24},{24,8},{8,0},{1,17},{17,25},{25,9},{9,1},{2,18},{18... | collective-permute-start | bytes 1179656 | tf_op jit(solution)/shard_map/ppermute | solution.py:32
  56.4 12.6 %collective-permute-start.10 = (f32[512]{0:T(512)S(1)}, f32[512]{0:T(512)S(1)}, u32[]{:S(2)}, u32[]{:S(2)}) collective-permute-start(f32[512]{0:T(512)S(1)} %pad_maximum_fusion), channel_id=1, source_target_pairs={{0,24},{16,8},{24,0},{8,16},{1,25},{17,9},{25,1},{9,17},{2,26},{18... | collective-permute-start | bytes 6152 | tf_op jit(solution)/shard_map/ppermute | solution.py:32
  59.0 6.2 %collective-permute-start.2 = (f32[64,896]{1,0:T(8,128)S(1)}, f32[64,896]{1,0:T(8,128)S(1)}, u32[]{:S(2)}, u32[]{:S(2)}) collective-permute-start(f32[64,896]{1,0:T(8,128)S(1)} %slice.54), channel_id=1, source_target_pairs={{0,4},{1,5},{2,6},{3,7},{4,0},{5,1},{6,2},{7,3},{8,12},{9,13},{10,... | collective-permute-start | bytes 688136 | tf_op jit(solution)/shard_map/ppermute | solution.py:37
  64.0 10.0 %collective-permute-start.13 = (f32[512]{0:T(512)S(1)}, f32[512]{0:T(512)S(1)}, u32[]{:S(2)}, u32[]{:S(2)}) collective-permute-start(f32[512]{0:T(512)S(1)} %pad_maximum_fusion.1), channel_id=1, source_target_pairs={{0,16},{16,24},{24,8},{8,0},{1,17},{17,25},{25,9},{9,1},{2,18},{18... | collective-permute-start | bytes 6152 | tf_op jit(solution)/shard_map/ppermute | solution.py:32
  65.3 3.9 %collective-permute-start.3 = (bf16[16,896]{1,0:T(8,128)(2,1)S(1)}, bf16[16,896]{1,0:T(8,128)(2,1)S(1)}, u32[]{:S(2)}, u32[]{:S(2)}) collective-permute-start(bf16[16,896]{1,0:T(8,128)(2,1)S(1)} %get-tuple-element.23), channel_id=1, source_target_pairs={{0,16},{16,24},{24,8},{8,0},{1,17},{17,25},{25,9},{9,1},{2,18},{18... | collective-permute-start | bytes 86024 | tf_op jit(solution)/shard_map/ppermute | solution.py:32
  67.2 5.7 %collective-permute-start.4 = (bf16[16,896]{1,0:T(8,128)(2,1)S(1)}, bf16[16,896]{1,0:T(8,128)(2,1)S(1)}, u32[]{:S(2)}, u32[]{:S(2)}) collective-permute-start(bf16[16,896]{1,0:T(8,128)(2,1)S(1)} %get-tuple-element.22), channel_id=1, source_target_pairs={{0,24},{16,8},{24,0},{8,16},{1,25},{17,9},{25,1},{9,17},{2,26},{18... | collective-permute-start | bytes 86024 | tf_op jit(solution)/shard_map/ppermute | solution.py:32
  68.5 4.8 %collective-permute-start.5 = (bf16[16,896]{1,0:T(8,128)(2,1)S(1)}, bf16[16,896]{1,0:T(8,128)(2,1)S(1)}, u32[]{:S(2)}, u32[]{:S(2)}) collective-permute-start(bf16[16,896]{1,0:T(8,128)(2,1)S(1)} %get-tuple-element.21), channel_id=1, source_target_pairs={{0,8},{16,0},{24,16},{8,24},{1,9},{17,1},{25,17},{9,25},{2,10},{18... | collective-permute-start | bytes 86024 | tf_op jit(solution)/shard_map/ppermute | solution.py:32

commit v6 on v5

--- a/solution.py
+++ b/solution.py
@@ -117,11 +117,12 @@
         ),
         name="prepare",
     )(
-        new_rows,
-        kept_row[None, :],
-        kept_owner[:, 0][None, :],
-        kept_local[None, :],
-        pattern.T,
+        pltpu.with_memory_space_constraint(new_rows, pltpu.HBM),
+        *[
+            pltpu.with_memory_space_constraint(value, pltpu.HBM)
+            for value in (kept_row[None, :], kept_owner[:, 0][None, :], kept_local[None, :])
+        ],
+        pltpu.with_memory_space_constraint(pattern.T, pltpu.HBM),
     )
 
 

time: 74.7 us -> 74.7 us (level)
  local copies, waits for them, and re-layouts: 4.03 us -> 1.15 us
  waiting for transfers between devices: 27.9 us -> 30.1 us
  Pallas kernels: 1.59 us -> 2.76 us
    unnamed x14 -> x4, local copies, waits for them, and re-layouts: 3.89 us -> 0.01 us
    ppermute x11, waiting for transfers between devices: 27.9 us -> 30.1 us  [shifted(): return lax.ppermute(value, axis, pairs)]
    pallas_call x1, Pallas kernels: 0.95 us -> 2.12 us  [prepare(): pl.pallas_call(lambda *refs: prepare_body(cycle, lanes, *refs), out_shape...]
    slice x1, local copies, waits for them, and re-layouts: 0.03 us -> 1.03 us  [per_device(): second = shifted(lax.optimization_barrier(new_rows)[half:], 'blk', -1)]
  transfers between devices with their start and end apart: 14 -> 14, of which waited for: 7 -> 7; matrix products, arithmetic and copies ran while one was open for 27% -> 28% of each run, Pallas kernels for 2% -> 4%
where the time goes in v6:
time: 74.7 us; the launch traced here: 74.5 us
  waiting for transfers between devices  30.1 us (40%)
  starting transfers between devices  19.5 us (26%)
  matrix products  15.3 us (20%)
  other arithmetic  4.89 us (7%)
  Pallas kernels  2.76 us (4%)
  local copies, waits for them, and re-layouts  1.15 us (2%)
  between operations  0.8 us (1%)
    ppermute x11, waiting for transfers between devices, shifted(): return lax.ppermute(value, axis, pairs)  30.1 us
    ppermute x11, starting transfers between devices, shifted(): return lax.ppermute(value, axis, pairs)  16.3 us
    dot_general x6, matrix products, tile_max(): lax.dot_general(block, index_rows, (((1,), (1,)), ((), ())), preferred_el...  15.3 us
    reduce_sum x1, other arithmetic, inverse_norm(): return lax.rsqrt(jnp.sum(wide * wide, axis=-1, keepdims=True) + EPS)  4.09 us
    ppermute x3, starting transfers between devices, swapped(): lax.ppermute(value, axis, [(source, source ^ bit) for source in range(cou...  3.21 us
    pallas_call x1, Pallas kernels, prepare(): pl.pallas_call(lambda *refs: prepare_body(cycle, lanes, *refs), out_shape...  2.12 us
  transfers between devices with their start and end apart: 14, of which 7 were waited for; matrix products, arithmetic and copies ran while one was open for 28% of the time, Pallas kernels for 4%

profile of v6, /device:TPU:0, one launch (start us, length us, event | category | flops | bytes accessed | tf_op | source)
XLA Modules:
  0.0 74.5 jit_solution(13819575004330440203)
XLA Ops:
  0.7 4.1 %collective-permute-start.6 = (bf16[512,768]{1,0:T(8,128)(2,1)}, bf16[512,768]{1,0:T(8,128)(2,1)S(1)}, u32[]{:S(2)}, u32[]{:S(2)}) collective-permute-start(bf16[512,768]{1,0:T(8,128)(2,1)} %refs_0_.1), channel_id=1, source_target_pairs={{0,16},{16,24},{24,8},{8,0},{1,17},{17,25},{25,9},{9,1},{2,18},{18... | collective-permute-start | bytes 2359304 | tf_op jit(solution)/shard_map/ppermute | solution.py:32
  4.8 2.1 %prepare.1 = (f32[256,896]{1,0:T(8,128)S(1)}, f32[256,896]{1,0:T(8,128)S(1)}, f32[1,512]{1,0:T(1,128)S(1)}, s32[4,512]{1,0:T(4,128)S(1)}) custom-call(bf16[512,768]{1,0:T(8,128)(2,1)} %refs_0_.1, s32[1,256]{1,0:T(1,128)} %bitcast.28, s32[1,256]{1,0:T(1,128)} %bitcast.29, s32[1,256]{1,0:T(1,128)} %bitcast.30, s32[4,32]{1,0:T(4,128)} %bitcast.27), custom_call_target="tpu_custom_call" | custom-call | flops 570425344 | bytes 2621440 | tf_op jit(solution)/shard_map/prepare/pallas_call | solution.py:104
  7.0 1.0 %slice.61 = bf16[256,768]{1,0:T(8,128)(2,1)S(1)} slice(bf16[512,768]{1,0:T(8,128)(2,1)} %refs_0_.1), slice={[256:512], [0:768]} | slice | bytes 786432 | tf_op jit(solution)/shard_map/slice | solution.py:196
  8.1 4.1 %multiply_reduce_fusion = f32[4096]{0:T(1024)S(1)} fusion(bf16[4096,768]{1,0:T(8,128)(2,1)} %param.7), kind=kLoop, calls=%fused_computation | loop fusion | flops 9433088 | bytes 6307840 | tf_op jit(solution)/shard_map/reduce_sum | solution.py:42
  12.2 3.8 %multiply_reduce_fusion.2 = f32[512]{0:T(512)S(1)} fusion(bf16[512,768]{1,0:T(8,128)(2,1)S(1)} %copy-done.1, bf16[4096,768]{1,0:T(8,128)(2,1)S(1)} %copy-done, f32[4096]{0:T(1024)S(1)} %add_rsqrt_fusion), kind=kOutput, calls=%fused_computation.2 | convolution fusion | flops 3225419264 | bytes 7096320 | tf_op jit(solution)/shard_map/dot_general | solution.py:186
  16.0 16.0 %collective-permute-done.12 = bf16[256,768]{1,0:T(8,128)(2,1)S(1)} collective-permute-done((bf16[256,768]{1,0:T(8,128)(2,1)S(1)}, bf16[256,768]{1,0:T(8,128)(2,1)S(1)}, u32[]{:S(2)}, u32[]{:S(2)}) %collective-permute-start.12) | collective-permute-done | bytes 393248 | tf_op jit(solution)/shard_map/ppermute | solution.py:32
  32.0 1.9 %fusion.3 = f32[256]{0:T(256)S(1)} fusion(f32[4096]{0:T(1024)S(1)} %add_rsqrt_fusion, bf16[256,768]{1,0:T(8,128)(2,1)S(1)} %collective-permute-done.12, bf16[4096,768]{1,0:T(8,128)(2,1)S(1)} %copy-done), kind=kOutput, calls=%fused_computation.10 | convolution fusion | flops 1612709632 | bytes 6702080 | tf_op jit(solution)/shard_map/dot_general | solution.py:186
  34.0 0.7 collective-permute-start.8
  34.7 2.4 %collective-permute-start.9 = (bf16[256,768]{1,0:T(8,128)(2,1)S(1)}, bf16[256,768]{1,0:T(8,128)(2,1)S(1)}, u32[]{:S(2)}, u32[]{:S(2)}) collective-permute-start(bf16[256,768]{1,0:T(8,128)(2,1)S(1)} %get-tuple-element.20), channel_id=1, source_target_pairs={{0,16},{16,24},{24,8},{8,0},{1,17},{17,25},{25,9},{9,1},{2,18},{18... | collective-permute-start | bytes 1179656 | tf_op jit(solution)/shard_map/ppermute | solution.py:32
  37.1 3.8 %multiply_reduce_fusion.1 = f32[512]{0:T(512)S(1)} fusion(bf16[512,768]{1,0:T(8,128)(2,1)S(1)} %collective-permute-done.6, bf16[4096,768]{1,0:T(8,128)(2,1)S(1)} %copy-done, f32[4096]{0:T(1024)S(1)} %add_rsqrt_fusion), kind=kOutput, calls=%fused_computation.1 | convolution fusion | flops 3225419264 | bytes 7096320 | tf_op jit(solution)/shard_map/dot_general | solution.py:186
  41.1 1.6 %collective-permute-start.1 = (f32[128,896]{1,0:T(8,128)S(1)}, f32[128,896]{1,0:T(8,128)S(1)}, u32[]{:S(2)}, u32[]{:S(2)}) collective-permute-start(f32[128,896]{1,0:T(8,128)S(1)} %slice.52), channel_id=1, source_target_pairs={{0,2},{1,3},{2,0},{3,1},{4,6},{5,7},{6,4},{7,5},{8,10},{9,11},{10,... | collective-permute-start | bytes 1376264 | tf_op jit(solution)/shard_map/ppermute | solution.py:37
  42.7 3.4 %collective-permute-done.8 = bf16[256,768]{1,0:T(8,128)(2,1)S(1)} collective-permute-done((bf16[256,768]{1,0:T(8,128)(2,1)S(1)}, bf16[256,768]{1,0:T(8,128)(2,1)S(1)}, u32[]{:S(2)}, u32[]{:S(2)}) %collective-permute-start.8) | collective-permute-done | bytes 393248 | tf_op jit(solution)/shard_map/ppermute | solution.py:32
  46.1 1.5 %collective-permute-start.11 = (bf16[256,768]{1,0:T(8,128)(2,1)S(1)}, bf16[256,768]{1,0:T(8,128)(2,1)S(1)}, u32[]{:S(2)}, u32[]{:S(2)}) collective-permute-start(bf16[256,768]{1,0:T(8,128)(2,1)S(1)} %collective-permute-done.8), channel_id=1, source_target_pairs={{0,16},{16,24},{24,8},{8,0},{1,17},{17,25},{25,9},{9,1},{2,18},{18... | collective-permute-start | bytes 1179656 | tf_op jit(solution)/shard_map/ppermute | solution.py:32
  47.6 1.9 %fusion = f32[256]{0:T(256)S(1)} fusion(f32[4096]{0:T(1024)S(1)} %add_rsqrt_fusion, bf16[256,768]{1,0:T(8,128)(2,1)S(1)} %collective-permute-done.8, bf16[4096,768]{1,0:T(8,128)(2,1)S(1)} %copy-done), kind=kOutput, calls=%fused_computation.7 | convolution fusion | flops 1612709632 | bytes 6702080 | tf_op jit(solution)/shard_map/dot_general | solution.py:186
  49.5 5.0 %collective-permute-done.9 = bf16[256,768]{1,0:T(8,128)(2,1)S(1)} collective-permute-done((bf16[256,768]{1,0:T(8,128)(2,1)S(1)}, bf16[256,768]{1,0:T(8,128)(2,1)S(1)}, u32[]{:S(2)}, u32[]{:S(2)}) %collective-permute-start.9) | collective-permute-done | bytes 393248 | tf_op jit(solution)/shard_map/ppermute | solution.py:32
  54.5 1.9 %fusion.1 = f32[256]{0:T(256)S(1)} fusion(f32[4096]{0:T(1024)S(1)} %add_rsqrt_fusion, bf16[256,768]{1,0:T(8,128)(2,1)S(1)} %collective-permute-done.9, bf16[4096,768]{1,0:T(8,128)(2,1)S(1)} %copy-done), kind=kOutput, calls=%fused_computation.8 | convolution fusion | flops 1612709632 | bytes 6702080 | tf_op jit(solution)/shard_map/dot_general | solution.py:186
  56.4 2.5 %collective-permute-start.10 = (f32[512]{0:T(512)S(1)}, f32[512]{0:T(512)S(1)}, u32[]{:S(2)}, u32[]{:S(2)}) collective-permute-start(f32[512]{0:T(512)S(1)} %pad_maximum_fusion), channel_id=1, source_target_pairs={{0,24},{16,8},{24,0},{8,16},{1,25},{17,9},{25,1},{9,17},{2,26},{18... | collective-permute-start | bytes 6152 | tf_op jit(solution)/shard_map/ppermute | solution.py:32
  59.0 1.6 %collective-permute-start.2 = (f32[64,896]{1,0:T(8,128)S(1)}, f32[64,896]{1,0:T(8,128)S(1)}, u32[]{:S(2)}, u32[]{:S(2)}) collective-permute-start(f32[64,896]{1,0:T(8,128)S(1)} %slice.54), channel_id=1, source_target_pairs={{0,4},{1,5},{2,6},{3,7},{4,0},{5,1},{6,2},{7,3},{8,12},{9,13},{10,... | collective-permute-start | bytes 688136 | tf_op jit(solution)/shard_map/ppermute | solution.py:37
  60.6 1.4 %collective-permute-done.11 = bf16[256,768]{1,0:T(8,128)(2,1)S(1)} collective-permute-done((bf16[256,768]{1,0:T(8,128)(2,1)S(1)}, bf16[256,768]{1,0:T(8,128)(2,1)S(1)}, u32[]{:S(2)}, u32[]{:S(2)}) %collective-permute-start.11) | collective-permute-done | bytes 393248 | tf_op jit(solution)/shard_map/ppermute | solution.py:32
  62.1 1.9 %fusion.2 = f32[256]{0:T(256)S(1)} fusion(f32[4096]{0:T(1024)S(1)} %add_rsqrt_fusion, bf16[256,768]{1,0:T(8,128)(2,1)S(1)} %collective-permute-done.11, bf16[4096,768]{1,0:T(8,128)(2,1)S(1)} %copy-done), kind=kOutput, calls=%fused_computation.9 | convolution fusion | flops 1612709632 | bytes 6702080 | tf_op jit(solution)/shard_map/dot_general | solution.py:186
  64.0 1.3 %collective-permute-start.13 = (f32[512]{0:T(512)S(1)}, f32[512]{0:T(512)S(1)}, u32[]{:S(2)}, u32[]{:S(2)}) collective-permute-start(f32[512]{0:T(512)S(1)} %pad_maximum_fusion.1), channel_id=1, source_target_pairs={{0,16},{16,24},{24,8},{8,0},{1,17},{17,25},{25,9},{9,1},{2,18},{18... | collective-permute-start | bytes 6152 | tf_op jit(solution)/shard_map/ppermute | solution.py:32
  65.3 1.9 %collective-permute-start.3 = (bf16[16,896]{1,0:T(8,128)(2,1)S(1)}, bf16[16,896]{1,0:T(8,128)(2,1)S(1)}, u32[]{:S(2)}, u32[]{:S(2)}) collective-permute-start(bf16[16,896]{1,0:T(8,128)(2,1)S(1)} %get-tuple-element.23), channel_id=1, source_target_pairs={{0,16},{16,24},{24,8},{8,0},{1,17},{17,25},{25,9},{9,1},{2,18},{18... | collective-permute-start | bytes 86024 | tf_op jit(solution)/shard_map/ppermute | solution.py:32
  67.2 1.3 %collective-permute-start.4 = (bf16[16,896]{1,0:T(8,128)(2,1)S(1)}, bf16[16,896]{1,0:T(8,128)(2,1)S(1)}, u32[]{:S(2)}, u32[]{:S(2)}) collective-permute-start(bf16[16,896]{1,0:T(8,128)(2,1)S(1)} %get-tuple-element.22), channel_id=1, source_target_pairs={{0,24},{16,8},{24,0},{8,16},{1,25},{17,9},{25,1},{9,17},{2,26},{18... | collective-permute-start | bytes 86024 | tf_op jit(solution)/shard_map/ppermute | solution.py:32
  69.2 3.6 %collective-permute-done.4.refs_2_ = bf16[16,896]{1,0:T(8,128)(2,1)S(1)} collective-permute-done((bf16[16,896]{1,0:T(8,128)(2,1)S(1)}, bf16[16,896]{1,0:T(8,128)(2,1)S(1)}, u32[]{:S(2)}, u32[]{:S(2)}) %collective-permute-start.4) | collective-permute-done | bytes 28704 | tf_op jit(solution)/shard_map/ppermute | solution.py:32
  (31 shorter events, 2.9 us)
Async XLA Ops:
  0.6 11.6 %copy-start.1 = (bf16[512,768]{1,0:T(8,128)(2,1)S(1)}, bf16[512,768]{1,0:T(8,128)(2,1)}, u32[]{:S(2)}) copy-start(bf16[512,768]{1,0:T(8,128)(2,1)} %refs_0_.1) | copy-start | bytes 2359300
  0.6 11.5 %copy-start = (bf16[4096,768]{1,0:T(8,128)(2,1)S(1)}, bf16[4096,768]{1,0:T(8,128)(2,1)}, u32[]{:S(2)}) copy-start(bf16[4096,768]{1,0:T(8,128)(2,1)} %param.7) | copy-start | bytes 18874372
  0.7 33.3 %collective-permute-start.6 = (bf16[512,768]{1,0:T(8,128)(2,1)}, bf16[512,768]{1,0:T(8,128)(2,1)S(1)}, u32[]{:S(2)}, u32[]{:S(2)}) collective-permute-start(bf16[512,768]{1,0:T(8,128)(2,1)} %refs_0_.1), channel_id=1, source_target_pairs={{0,16},{16,24},{24,8},{8,0},{1,17},{17,25},{25,9},{9,1},{2,18},{18... | collective-permute-start | bytes 2359304 | tf_op jit(solution)/shard_map/ppermute | solution.py:32
  6.9 34.1 %collective-permute-start = (f32[256,896]{1,0:T(8,128)S(1)}, f32[256,896]{1,0:T(8,128)S(1)}, u32[]{:S(2)}, u32[]{:S(2)}) collective-permute-start(f32[256,896]{1,0:T(8,128)S(1)} %get-tuple-element.11), channel_id=1, source_target_pairs={{0,1},{1,0},{2,3},{3,2},{4,5},{5,4},{6,7},{7,6},{8,9},{9,8},{10,11... | collective-permute-start | bytes 2752520 | tf_op jit(solution)/shard_map/ppermute | solution.py:37
  8.0 24.0 %collective-permute-start.12 = (bf16[256,768]{1,0:T(8,128)(2,1)S(1)}, bf16[256,768]{1,0:T(8,128)(2,1)S(1)}, u32[]{:S(2)}, u32[]{:S(2)}) collective-permute-start(bf16[256,768]{1,0:T(8,128)(2,1)S(1)} %slice.61), channel_id=1, source_target_pairs={{0,8},{16,0},{24,16},{8,24},{1,9},{17,1},{25,17},{9,25},{2,10},{18... | collective-permute-start | bytes 1179656 | tf_op jit(solution)/shard_map/ppermute | solution.py:32
  34.0 12.1 %collective-permute-start.8 = (bf16[256,768]{1,0:T(8,128)(2,1)S(1)}, bf16[256,768]{1,0:T(8,128)(2,1)S(1)}, u32[]{:S(2)}, u32[]{:S(2)}) collective-permute-start(bf16[256,768]{1,0:T(8,128)(2,1)S(1)} %get-tuple-element.19), channel_id=1, source_target_pairs={{0,16},{16,24},{24,8},{8,0},{1,17},{17,25},{25,9},{9,1},{2,18},{18... | collective-permute-start | bytes 1179656 | tf_op jit(solution)/shard_map/ppermute | solution.py:32
  34.7 19.8 %collective-permute-start.9 = (bf16[256,768]{1,0:T(8,128)(2,1)S(1)}, bf16[256,768]{1,0:T(8,128)(2,1)S(1)}, u32[]{:S(2)}, u32[]{:S(2)}) collective-permute-start(bf16[256,768]{1,0:T(8,128)(2,1)S(1)} %get-tuple-element.20), channel_id=1, source_target_pairs={{0,16},{16,24},{24,8},{8,0},{1,17},{17,25},{25,9},{9,1},{2,18},{18... | collective-permute-start | bytes 1179656 | tf_op jit(solution)/shard_map/ppermute | solution.py:32
  40.9 27.6 %collective-permute-start.7 = (f32[512]{0:T(512)S(1)}, f32[512]{0:T(512)S(1)}, u32[]{:S(2)}, u32[]{:S(2)}) collective-permute-start(f32[512]{0:T(512)S(1)} %multiply_reduce_fusion.1), channel_id=1, source_target_pairs={{0,8},{16,0},{24,16},{8,24},{1,9},{17,1},{25,17},{9,25},{2,10},{18... | collective-permute-start | bytes 6152 | tf_op jit(solution)/shard_map/ppermute | solution.py:32
  41.1 17.8 %collective-permute-start.1 = (f32[128,896]{1,0:T(8,128)S(1)}, f32[128,896]{1,0:T(8,128)S(1)}, u32[]{:S(2)}, u32[]{:S(2)}) collective-permute-start(f32[128,896]{1,0:T(8,128)S(1)} %slice.52), channel_id=1, source_target_pairs={{0,2},{1,3},{2,0},{3,1},{4,6},{5,7},{6,4},{7,5},{8,10},{9,11},{10,... | collective-permute-start | bytes 1376264 | tf_op jit(solution)/shard_map/ppermute | solution.py:37
  46.1 16.0 %collective-permute-start.11 = (bf16[256,768]{1,0:T(8,128)(2,1)S(1)}, bf16[256,768]{1,0:T(8,128)(2,1)S(1)}, u32[]{:S(2)}, u32[]{:S(2)}) collective-permute-start(bf16[256,768]{1,0:T(8,128)(2,1)S(1)} %collective-permute-done.8), channel_id=1, source_target_pairs={{0,16},{16,24},{24,8},{8,0},{1,17},{17,25},{25,9},{9,1},{2,18},{18... | collective-permute-start | bytes 1179656 | tf_op jit(solution)/shard_map/ppermute | solution.py:32
  56.4 12.6 %collective-permute-start.10 = (f32[512]{0:T(512)S(1)}, f32[512]{0:T(512)S(1)}, u32[]{:S(2)}, u32[]{:S(2)}) collective-permute-start(f32[512]{0:T(512)S(1)} %pad_maximum_fusion), channel_id=1, source_target_pairs={{0,24},{16,8},{24,0},{8,16},{1,25},{17,9},{25,1},{9,17},{2,26},{18... | collective-permute-start | bytes 6152 | tf_op jit(solution)/shard_map/ppermute | solution.py:32
  59.0 6.2 %collective-permute-start.2 = (f32[64,896]{1,0:T(8,128)S(1)}, f32[64,896]{1,0:T(8,128)S(1)}, u32[]{:S(2)}, u32[]{:S(2)}) collective-permute-start(f32[64,896]{1,0:T(8,128)S(1)} %slice.54), channel_id=1, source_target_pairs={{0,4},{1,5},{2,6},{3,7},{4,0},{5,1},{6,2},{7,3},{8,12},{9,13},{10,... | collective-permute-start | bytes 688136 | tf_op jit(solution)/shard_map/ppermute | solution.py:37
  64.0 10.0 %collective-permute-start.13 = (f32[512]{0:T(512)S(1)}, f32[512]{0:T(512)S(1)}, u32[]{:S(2)}, u32[]{:S(2)}) collective-permute-start(f32[512]{0:T(512)S(1)} %pad_maximum_fusion.1), channel_id=1, source_target_pairs={{0,16},{16,24},{24,8},{8,0},{1,17},{17,25},{25,9},{9,1},{2,18},{18... | collective-permute-start | bytes 6152 | tf_op jit(solution)/shard_map/ppermute | solution.py:32
  65.3 3.9 %collective-permute-start.3 = (bf16[16,896]{1,0:T(8,128)(2,1)S(1)}, bf16[16,896]{1,0:T(8,128)(2,1)S(1)}, u32[]{:S(2)}, u32[]{:S(2)}) collective-permute-start(bf16[16,896]{1,0:T(8,128)(2,1)S(1)} %get-tuple-element.23), channel_id=1, source_target_pairs={{0,16},{16,24},{24,8},{8,0},{1,17},{17,25},{25,9},{9,1},{2,18},{18... | collective-permute-start | bytes 86024 | tf_op jit(solution)/shard_map/ppermute | solution.py:32
  67.2 5.7 %collective-permute-start.4 = (bf16[16,896]{1,0:T(8,128)(2,1)S(1)}, bf16[16,896]{1,0:T(8,128)(2,1)S(1)}, u32[]{:S(2)}, u32[]{:S(2)}) collective-permute-start(bf16[16,896]{1,0:T(8,128)(2,1)S(1)} %get-tuple-element.22), channel_id=1, source_target_pairs={{0,24},{16,8},{24,0},{8,16},{1,25},{17,9},{25,1},{9,17},{2,26},{18... | collective-permute-start | bytes 86024 | tf_op jit(solution)/shard_map/ppermute | solution.py:32
  68.5 4.8 %collective-permute-start.5 = (bf16[16,896]{1,0:T(8,128)(2,1)S(1)}, bf16[16,896]{1,0:T(8,128)(2,1)S(1)}, u32[]{:S(2)}, u32[]{:S(2)}) collective-permute-start(bf16[16,896]{1,0:T(8,128)(2,1)S(1)} %get-tuple-element.21), channel_id=1, source_target_pairs={{0,8},{16,0},{24,16},{8,24},{1,9},{17,1},{25,17},{9,25},{2,10},{18... | collective-permute-start | bytes 86024 | tf_op jit(solution)/shard_map/ppermute | solution.py:32
